TPU v7x, 128 devices: a whole 4x4x4 slice. The times are simulated.
128 devices in a mesh: lat: 16 (over z_hi, y, core), lon: 8 (over x, z_lo).
Axes of the slice: x: 4, y: 4, z: 4 (z_hi: 2, z_lo: 2; z = z_hi * 2 + z_lo), core: 2. Of those that a mesh axis runs over, the one named last changes fastest.
Arguments:
- spectral: bfloat16 [6, 64, 640, 1280], P(None, 'lon', 'lat'), may hold values from -6 to 6
- legendre: bfloat16 [640, 1280, 256], P('lat'), may hold values from -0.15625 to 0.15625
- wave_ids: int32 [640], replicated, may hold values from 0 to 639, each once
- points: int32 [256], P('lat'), may hold values from 1024 to 2048
- tracers: bfloat16 [16, 64, 256, 2048], P(None, None, 'lat', 'lon'), may hold values from -6 to 6
- react_base: float32 [16, 16], replicated, may hold values from -0.75 to 0.75
- react_temp: float32 [16, 16], replicated, may hold values from -0.75 to 0.75
- active_ids: int32 [4], replicated, may hold values from 0 to 15, as said below
Outputs:
- tracers_new: bfloat16 [16, 64, 256, 2048], P(None, None, 'lat', 'lon')
- active: float32 [4, 64, 256, 2048], P(None, 'lon', 'lat')
Inputs may be any that keep to these rules, and one draw needn't show every extreme that they name: `active_ids`: distinct tracer indices. `wave_ids`: each slot a different wavenumber.
All inputs are finite; a program needn't handle non-finite values.
Results may differ from a plain program's by a relative error of at most 0.0042.
Values may be sent and summed in bfloat16 or wider, within the bound.
A program may use at most 256 MiB of HBM per device.

v0:
```python
import functools

import jax
import jax.numpy as jnp
from jax import lax
from jax.experimental import pallas as pl
from jax.experimental.pallas import tpu as pltpu
from jax.sharding import PartitionSpec as P

LON = "lon"


SRC = 16
DST = 8
MESH = pl.DeviceIdType.MESH
COS = (0.9999999888947231, -19.739204440276147, 64.93911426452443, -85.45007790017918,
       60.167101643628186, -25.965527386763885, 6.525643976222309)
SIN = (6.283185302441191, -41.34170037999709, 81.60513001863838, -76.70298898514991,
       42.02570052333535, -14.898960232258009, 3.2368479099117575)


def waves_at(product, count, inverse):
    turns = jnp.round(product * inverse)
    t = (product - turns * count) * inverse
    s = t * t
    c = COS[-1]
    for k in COS[-2::-1]:
        c = c * s + k
    d = SIN[-1]
    for k in SIN[-2::-1]:
        d = d * s + k
    return c, d * t


def spectral_kernel(
    four_ref, rowid_ref, laneid_ref, pts_ref,
    out_ref,
    tall, send_a, got_a, table, phase, coef, line, turned, send_b,
    sent_a, came_a, sent_b, came_b, own,
):
    g, h = lax.axis_index("lat"), lax.axis_index("lon")
    barrier = pltpu.get_barrier_semaphore()
    for d in range(1, SRC):
        pl.semaphore_signal(barrier, inc=1, device_id=(lax.rem(g + d, SRC), h), device_id_type=MESH)
    for d in range(1, DST):
        pl.semaphore_signal(barrier, inc=1, device_id=(g, lax.rem(h + d, DST)), device_id_type=MESH)

    for k in range(2):
        tall[k] = four_ref[:, :, 128 * k : 128 * k + 128].reshape(1920, 128).astype(jnp.float32)
    blank = jnp.zeros((8, 128), jnp.float32)

    def turn(r, carry):
        for k in range(2):
            parts = [tall[k, pl.ds(16 * f + r, 40, stride=48), :] for f in range(3)]
            block = jnp.concatenate(parts + [blank], axis=0).T.astype(jnp.bfloat16)
            for b in range(8):
                send_a[8 * k + b, r] = block[16 * b : 16 * b + 16]
        return carry

    lax.fori_loop(0, 16, turn, 0)
    pl.semaphore_wait(barrier, SRC + DST - 2)

    def copy_a(d):
        to = lax.rem(g + d, SRC)
        return pltpu.make_async_remote_copy(
            src_ref=send_a.at[to], dst_ref=got_a.at[g], send_sem=sent_a.at[d], recv_sem=came_a.at[d],
            device_id=(to, h), device_id_type=MESH,
        )

    for d in range(1, SRC):
        copy_a(d).start()
    mine = pltpu.make_async_copy(send_a.at[g], got_a.at[g], own.at[0])
    mine.start()

    shape = (128, 128)

    def tables(j, carry):
        count = jnp.full((1, 1), pts_ref[j], jnp.int32).astype(jnp.float32)
        inverse = 1.0 / count
        far = lax.broadcasted_iota(jnp.int32, (8, 128), 0).astype(jnp.float32) * 256.0
        lane = lax.broadcasted_iota(jnp.int32, shape, 1).astype(jnp.float32)
        for p in range(6):
            ids = laneid_ref[:, pl.ds(128 * p, 128)]
            c, s = waves_at(ids * far, count, inverse)
            phase[j, 0, p] = c
            phase[j, 1, p] = s
        for p in range(6):
            ids = rowid_ref[pl.ds(128 * p, 128), :]
            c, s = waves_at(ids * lane, count, inverse)
            c1, s1 = waves_at(ids * 128.0, count, inverse)
            table[j, pl.ds(128 * p, 128), pl.ds(0, 128)] = c.astype(jnp.bfloat16)
            table[j, pl.ds(768 + 128 * p, 128), pl.ds(0, 128)] = (-s).astype(jnp.bfloat16)
            table[j, pl.ds(128 * p, 128), pl.ds(128, 128)] = (c * c1 - s * s1).astype(jnp.bfloat16)
            table[j, pl.ds(768 + 128 * p, 128), pl.ds(128, 128)] = (-(s * c1 + c * s1)).astype(jnp.bfloat16)
        return carry

    lax.fori_loop(0, 16, tables, 0)

    mine.wait()
    for d in range(1, SRC):
        copy_a(d).wait_recv()

    def widen(q, carry):
        coef[pl.ds(256 * q, 256), :] = got_a[q].reshape(256, 128).astype(jnp.float32)
        return carry

    lax.fori_loop(0, SRC, widen, 0)

    def turn_of(j):
        lane = lax.broadcasted_iota(jnp.int32, (16, 128), 1)
        for p in range(6):
            held = []
            for q in range(3):
                s = 3 * p + q
                if s < SRC:
                    held.append(coef[pl.ds(256 * s + j, 16, stride=16), :])
                else:
                    held.append(None)
            for f in range(3):
                value = jnp.zeros((16, 128), jnp.float32)
                for q in range(3):
                    if held[q] is None:
                        continue
                    moved = held[q] if q == f else pltpu.roll(held[q], (40 * (q - f)) % 128, 1)
                    value = jnp.where((lane >= 40 * q) & (lane < 40 * q + 40), moved, value)
                re, im = value[:8], value[8:]
                line[f, 0, p] = re
                line[f, 1, p] = im
        for p in range(6):
            for a in range(0, DST, 2):
                parts = []
                for b in range(6):
                    row, f = a + b // 3, b % 3
                    c = phase[j, 0, p, row : row + 1, :]
                    s = phase[j, 1, p, row : row + 1, :]
                    re, im = line[f, 0, p], line[f, 1, p]
                    parts.append((re * c - im * s, re * s + im * c))
                for b in range(0, 6, 2):
                    at = 24 * a + 8 * b
                    for k in range(2):
                        pair = jnp.concatenate([parts[b][k], parts[b + 1][k]], axis=0)
                        turned[at : at + 16, 768 * k + 128 * p : 768 * k + 128 * p + 128] = pair.astype(jnp.bfloat16)
        out = jnp.dot(turned[...], table[j], preferred_element_type=jnp.float32)
        return out * (640.0 ** -0.5)

    def copy_b(d, c):
        to = lax.rem(h + d, DST)
        return pltpu.make_async_remote_copy(
            src_ref=send_b.at[c, to], dst_ref=out_ref.at[h, pl.ds(96 * c, 96), :],
            send_sem=sent_b.at[c, d], recv_sem=came_b.at[c, d], device_id=(g, to), device_id_type=MESH,
        )

    def copy_own(c):
        return pltpu.make_async_copy(send_b.at[c, h], out_ref.at[h, pl.ds(96 * c, 96), :], own.at[1 + c])

    def quad(c, carry):
        for jj in range(2):
            one = turn_of(4 * c + 2 * jj)
            two = turn_of(4 * c + 2 * jj + 1)
            for a in range(DST):
                both = jnp.concatenate([one[24 * a : 24 * a + 24], two[24 * a : 24 * a + 24]], axis=0)
                send_b[c, a, pl.ds(48 * jj, 48), :] = both.astype(jnp.bfloat16)
        for d in range(1, DST):
            copy_b(d, c).start()
        copy_own(c).start()
        return carry

    lax.fori_loop(0, 4, quad, 0)
    for d in range(1, SRC):
        copy_a(d).wait_send()

    def finish(c, carry):
        copy_own(c).wait()
        for d in range(1, DST):
            copy_b(d, c).wait()
        return carry

    lax.fori_loop(0, 4, finish, 0)


def winds_of(fourier, wave_ids, points):
    ids = jnp.zeros((6, 3, 40), jnp.float32).reshape(18, 40).at[:16].set(wave_ids.reshape(16, 40).astype(jnp.float32))
    ids = jnp.pad(ids.reshape(6, 120), ((0, 0), (0, 8))).reshape(768)
    rowid = jnp.broadcast_to(ids[:, None], (768, 128))
    laneid = jnp.broadcast_to(ids[None, :], (8, 768))
    vmem = pl.BlockSpec(memory_space=pltpu.VMEM)
    return pl.pallas_call(
        spectral_kernel,
        in_specs=[vmem, vmem, vmem, pl.BlockSpec(memory_space=pltpu.SMEM)],
        out_specs=pl.BlockSpec(memory_space=pl.ANY),
        out_shape=jax.ShapeDtypeStruct((8, 384, 256), jnp.bfloat16),
        scratch_shapes=[
            pltpu.VMEM((2, 1920, 128), jnp.float32),
            pltpu.VMEM((16, 16, 16, 128), jnp.bfloat16),
            pltpu.VMEM((16, 16, 16, 128), jnp.bfloat16),
            pltpu.VMEM((16, 1536, 256), jnp.bfloat16),
            pltpu.VMEM((16, 2, 6, 8, 128), jnp.float32),
            pltpu.VMEM((4096, 128), jnp.float32),
            pltpu.VMEM((3, 2, 6, 8, 128), jnp.float32),
            pltpu.VMEM((192, 1536), jnp.bfloat16),
            pltpu.VMEM((4, 8, 96, 256), jnp.bfloat16),
            pltpu.SemaphoreType.DMA((16,)),
            pltpu.SemaphoreType.DMA((16,)),
            pltpu.SemaphoreType.DMA((4, 8)),
            pltpu.SemaphoreType.DMA((4, 8)),
            pltpu.SemaphoreType.DMA((5,)),
        ],
        compiler_params=pltpu.CompilerParams(
            collective_id=0, has_side_effects=True, vmem_limit_bytes=60 * 1024 * 1024
        ),
        name="winds",
    )(fourier, rowid, laneid, points)


def rows_of(ref, start, size, stride):
    return jnp.concatenate([ref[k, pl.ds(start, size, stride=stride), :] for k in range(2)], axis=1)


def edge_kernel(tr_ref, low_ref, high_ref, col_ref, wide, acc):
    h = pl.program_id(0)
    lane = lax.broadcasted_iota(jnp.int32, (256, 128), 1)

    @pl.when(h == 0)
    def _():
        acc[...] = jnp.zeros_like(acc)

    def level(l, carry):
        x = tr_ref[:, l].reshape(256, 256).astype(jnp.float32)
        for k in range(2):
            wide[k] = x[:, 128 * k : 128 * k + 128]
        low_ref[l] = rows_of(wide, 0, 16, 16).astype(jnp.bfloat16)
        high_ref[l] = rows_of(wide, 15, 16, 16).astype(jnp.bfloat16)
        at = h * 8 + l
        first = pltpu.roll(x[:, :128], at, 1)
        last = pltpu.roll(x[:, 128:], lax.rem(at + 65, 128), 1)
        acc[...] = jnp.where(lane == at, first, jnp.where(lane == at + 64, last, acc[...]))
        return carry

    lax.fori_loop(0, 8, level, 0)

    @pl.when(h == pl.num_programs(0) - 1)
    def _():
        col_ref[...] = acc[...].astype(jnp.bfloat16)


def edges_of(tracers):
    return pl.pallas_call(
        edge_kernel,
        grid=(8,),
        in_specs=[pl.BlockSpec((16, 8, 16, 256), lambda h: (0, h, 0, 0))],
        out_specs=[
            pl.BlockSpec((8, 16, 256), lambda h: (h, 0, 0)),
            pl.BlockSpec((8, 16, 256), lambda h: (h, 0, 0)),
            pl.BlockSpec((256, 128), lambda h: (0, 0)),
        ],
        out_shape=[
            jax.ShapeDtypeStruct((64, 16, 256), jnp.bfloat16),
            jax.ShapeDtypeStruct((64, 16, 256), jnp.bfloat16),
            jax.ShapeDtypeStruct((256, 128), jnp.bfloat16),
        ],
        scratch_shapes=[pltpu.VMEM((2, 256, 128), jnp.float32), pltpu.VMEM((256, 128), jnp.float32)],
        name="edges",
    )(tracers)


def chem_kernel(
    ids_ref, tr_ref, wind_ref, north_ref, south_ref, east_ref, west_ref, mask_ref, base_ref, temp_ref,
    out_ref, act_ref, wide, east, west, mix, moved, moved_b,
):
    h = pl.program_id(0)

    @pl.when(h == 0)
    def _():
        east[...] = east_ref[...].astype(jnp.float32)
        west[...] = west_ref[...].astype(jnp.float32)
        row = lax.broadcasted_iota(jnp.int32, (256, 16), 0)
        col = lax.broadcasted_iota(jnp.int32, (256, 16), 1)
        spread = jnp.where(row // 16 == col, 1.0, 0.0).astype(jnp.bfloat16)
        row = lax.broadcasted_iota(jnp.int32, (256, 256), 0)
        col = lax.broadcasted_iota(jnp.int32, (256, 256), 1)
        same = row % 16 == col % 16
        for k, ref in enumerate((base_ref, temp_ref)):
            rows = jnp.dot(spread, ref[...].astype(jnp.bfloat16), preferred_element_type=jnp.float32)
            full = lax.dot_general(
                rows.astype(jnp.bfloat16), spread, (((1,), (1,)), ((), ())), preferred_element_type=jnp.float32
            )
            mix[pl.ds(256 * k, 256), :] = jnp.where(same, full, 0.0).astype(jnp.bfloat16)

    for k in range(2):
        wide[k] = wind_ref[0, :, 128 * k : 128 * k + 128].astype(jnp.float32)
    lane = lax.broadcasted_iota(jnp.int32, (16, 128), 1)
    row = lax.broadcasted_iota(jnp.int32, (16, 256), 0)
    lane_low, lane_high = lane == 0, lane == 127
    row_low, row_high = row == 0, row == 15
    mask = mask_ref[...]

    def level(l, carry):
        at = h * 8 + l
        u = 0.1 * rows_of(wide, l, 16, 24)
        v = 0.1 * rows_of(wide, 8 + l, 16, 24)
        temper = rows_of(wide, 16 + l, 16, 24)
        east_w, west_w = 0.05 - u, 0.05 + u
        north_w, south_w = 0.05 - v, 0.05 + v
        north = north_ref[l].astype(jnp.float32)
        south = south_ref[l].astype(jnp.float32)
        for t in range(16):
            x = tr_ref[t, l].astype(jnp.float32)
            xl, xr = x[:, :128], x[:, 128:]
            he = pltpu.roll(east[pl.ds(16 * t, 16), :], 127 - at, 1)
            hw = pltpu.roll(west[pl.ds(16 * t, 16), :], 64 - at, 1)
            el, er = pltpu.roll(xl, 127, 1), pltpu.roll(xr, 127, 1)
            wl, wr = pltpu.roll(xl, 1, 1), pltpu.roll(xr, 1, 1)
            xe = jnp.concatenate([jnp.where(lane_high, er, el), jnp.where(lane_high, he, er)], axis=1)
            xw = jnp.concatenate([jnp.where(lane_low, hw, wl), jnp.where(lane_low, wl, wr)], axis=1)
            xn = jnp.where(row_high, north[t : t + 1, :], pltpu.roll(x, 15, 0))
            xs = jnp.where(row_low, south[t : t + 1, :], pltpu.roll(x, 1, 0))
            q = 0.8 * x + east_w * xe + west_w * xw + north_w * xn + south_w * xs
            moved[t] = q
            moved_b[pl.ds(16 * t, 16), :] = q.astype(jnp.bfloat16)
        y = jnp.dot(mix[...], moved_b[...], preferred_element_type=jnp.float32)
        for t in range(16):
            q = (moved[t] + y[16 * t : 16 * t + 16] + temper * y[256 + 16 * t : 272 + 16 * t]) * mask
            moved[t] = q
            out_ref[t, l] = q.astype(jnp.bfloat16)
        for a in range(4):
            act_ref[0, a, l] = moved[ids_ref[a]].astype(jnp.bfloat16)
        return carry

    lax.fori_loop(0, 8, level, 0)


def chemistry(tracers, winds, north, south, east, west, mask, base, temp, ids):
    whole = lambda h, i: (0, 0)
    return pl.pallas_call(
        chem_kernel,
        grid_spec=pltpu.PrefetchScalarGridSpec(
            num_scalar_prefetch=1,
            grid=(8,),
            in_specs=[
                pl.BlockSpec((16, 8, 16, 256), lambda h, i: (0, h, 0, 0)),
                pl.BlockSpec((1, 384, 256), lambda h, i: (h, 0, 0)),
                pl.BlockSpec((8, 16, 256), lambda h, i: (h, 0, 0)),
                pl.BlockSpec((8, 16, 256), lambda h, i: (h, 0, 0)),
                pl.BlockSpec((256, 128), whole),
                pl.BlockSpec((256, 128), whole),
                pl.BlockSpec((16, 256), whole),
                pl.BlockSpec((16, 16), whole),
                pl.BlockSpec((16, 16), whole),
            ],
            out_specs=[
                pl.BlockSpec((16, 8, 16, 256), lambda h, i: (0, h, 0, 0)),
                pl.BlockSpec((1, 4, 8, 16, 256), lambda h, i: (h, 0, 0, 0, 0)),
            ],
            scratch_shapes=[
                pltpu.VMEM((2, 384, 128), jnp.float32),
                pltpu.VMEM((256, 128), jnp.float32),
                pltpu.VMEM((256, 128), jnp.float32),
                pltpu.VMEM((512, 256), jnp.bfloat16),
                pltpu.VMEM((16, 16, 256), jnp.float32),
                pltpu.VMEM((256, 256), jnp.bfloat16),
            ],
        ),
        out_shape=[
            jax.ShapeDtypeStruct((16, 64, 16, 256), jnp.bfloat16),
            jax.ShapeDtypeStruct((8, 4, 8, 16, 256), jnp.bfloat16),
        ],
        name="chemistry",
    )(ids, tracers, winds, north, south, east, west, mask, base, temp)


def shifted(value, axis):
    size = lax.axis_size(axis)
    up = [(i, (i + 1) % size) for i in range(size - 1)]
    return lax.ppermute(value, axis, up)


def shifted_back(value, axis):
    size = lax.axis_size(axis)
    up = [((i + 1) % size, i) for i in range(size - 1)]
    return lax.ppermute(value, axis, up)


def body(spectral, legendre, wave_ids, points, tracers, react_base, react_temp, active_ids):
    low, high, cols = edges_of(tracers)
    south = shifted(high, "lat")
    north = shifted_back(low, "lat")
    west = shifted(cols, LON)
    east = shifted_back(cols, LON)
    fourier = lax.dot_general(
        spectral, legendre, (((3,), (1,)), ((2,), (0,))), preferred_element_type=jnp.float32
    )
    fourier = fourier.astype(jnp.bfloat16)
    winds = winds_of(fourier.reshape(40, 48, 256), wave_ids, points)
    columns = lax.axis_index("lon") * 256 + jnp.arange(256)
    mask = (columns[None, :] < points[:, None]).astype(jnp.float32)
    fresh, active = chemistry(
        tracers, winds, north, south, east, west, mask, react_base, react_temp, active_ids
    )
    active = lax.all_to_all(active, LON, split_axis=0, concat_axis=0, tiled=True)
    active = jnp.transpose(active, (1, 2, 3, 0, 4)).reshape(4, 8, 16, 2048).astype(jnp.float32)
    return (fresh, active)


def solution(mesh):
    in_specs = (
        P(None, LON, "lat", None),
        P("lat", None, None),
        P(),
        P("lat"),
        P(None, None, "lat", LON),
        P(),
        P(),
        P(),
    )
    out_specs = (P(None, None, "lat", LON), P(None, LON, "lat", None))
    return jax.shard_map(body, mesh=mesh, in_specs=in_specs, out_specs=out_specs, check_vma=False)
```

profile of v0, /device:TPU:25, one launch (start us, length us, event | category | flops | bytes accessed | tf_op | source)
XLA Modules:
  0.0 152.6 jit_solution(4930137703357435537)
XLA Ops:
  0.6 10.6 %edges.1 = (bf16[64,16,256]{2,1,0:T(8,128)(2,1)}, bf16[64,16,256]{2,1,0:T(8,128)(2,1)}, bf16[256,128]{1,0:T(8,128)(2,1)}) custom-call(bf16[16,64,16,256]{3,2,1,0:T(8,128)(2,1)} %tr_ref.3), custom_call_target="tpu_custom_call" | custom-call | tf_op jit(solution)/shard_map/edges/pallas_call | solution.py:247
  11.2 3.5 %collective-permute-start.3 = (bf16[256,128]{1,0:T(8,128)(2,1)}, bf16[256,128]{1,0:T(8,128)(2,1)S(1)}, u32[]{:S(2)}, u32[]{:S(2)}) collective-permute-start(bf16[256,128]{1,0:T(8,128)(2,1)} %get-tuple-element.21), channel_id=1, source_target_pairs={{0,1},{1,2},{2,3},{3,4},{4,5},{5,6},{6,7},{8,9},{9,10},{10,11},{11... | collective-permute-start | bytes 196616 | tf_op jit(solution)/shard_map/ppermute | solution.py:374
  14.8 1.3 collective-permute-start.2
  16.1 2.9 %collective-permute-start = (bf16[64,16,256]{2,1,0:T(8,128)(2,1)}, bf16[64,16,256]{2,1,0:T(8,128)(2,1)S(1)}, u32[]{:S(2)}, u32[]{:S(2)}) collective-permute-start(bf16[64,16,256]{2,1,0:T(8,128)(2,1)} %get-tuple-element.19), channel_id=1, source_target_pairs={{8,0},{16,8},{24,16},{32,24},{40,32},{48,40},{56,48},{64,56},{72,6... | collective-permute-start | bytes 1572872 | tf_op jit(solution)/shard_map/ppermute | solution.py:380
  18.9 0.0 copy-start.4
  18.9 0.0 copy-start.5
  19.0 6.3 %collective-permute-start.1 = (bf16[64,16,256]{2,1,0:T(8,128)(2,1)}, bf16[64,16,256]{2,1,0:T(8,128)(2,1)S(1)}, u32[]{:S(2)}, u32[]{:S(2)}) collective-permute-start(bf16[64,16,256]{2,1,0:T(8,128)(2,1)} %get-tuple-element.20), channel_id=1, source_target_pairs={{0,8},{8,16},{16,24},{24,32},{32,40},{40,48},{48,56},{56,64},{64,7... | collective-permute-start | bytes 1572872 | tf_op jit(solution)/shard_map/ppermute | solution.py:374
  25.3 14.7 %fusion.8.four_ref = bf16[40,48,256]{2,1,0:T(8,128)(2,1)} fusion(bf16[40,1280,256]{2,1,0:T(8,128)(2,1)} %param.11, bf16[6,8,40,1280]{3,2,1,0:T(8,128)(2,1)} %param.10), kind=kOutput, calls=%fused_computation.5 | convolution fusion | flops 1258782720 | bytes 32112640 | tf_op jit(solution)/shard_map/dot_general | solution.py:389
  39.9 0.0 copy-done.4
  40.0 0.1 convert_element_type.25
  40.1 0.1 reshape.50
  40.1 0.0 copy-done.5
  40.1 0.7 compare_convert_fusion.mask_ref
  40.8 0.6 broadcast_in_dim.16.laneid_ref
  41.4 0.9 broadcast_in_dim.7.rowid_ref
  42.3 44.6 %winds.1.wind_ref = bf16[8,384,256]{2,1,0:T(8,128)(2,1)} custom-call(bf16[40,48,256]{2,1,0:T(8,128)(2,1)} %fusion.8.four_ref, f32[768,128]{1,0:T(8,128)} %broadcast_in_dim.7.rowid_ref, f32[8,768]{1,0:T(8,128)} %broadcast_in_dim.16.laneid_ref, s32[16]{0:T(128)} %pts_ref.1), custom_call_target="tpu_custom_call" | custom-call | tf_op jit(solution)/shard_map/winds/pallas_call | solution.py:187
  86.9 0.0 collective-permute-done.3.west_ref
  86.9 0.0 copy-start.2
  86.9 0.0 collective-permute-done.2.east_ref
  86.9 0.0 copy-start.3
  87.0 0.0 collective-permute-done.north_ref
  87.0 0.0 copy-start
  87.0 0.0 collective-permute-done.1.south_ref
  87.0 0.6 copy-done.2
  87.6 0.0 copy-done.3
  87.6 0.2 copy-done
  87.8 0.0 copy-start.1
  87.8 0.8 copy-done.1
  88.6 31.3 %chemistry.1 = (bf16[16,64,16,256]{3,2,1,0:T(8,128)(2,1)}, bf16[8,4,8,16,256]{4,3,2,1,0:T(8,128)(2,1)}) custom-call(s32[4]{0:T(128)} %ids_ref.1, bf16[16,64,16,256]{3,2,1,0:T(8,128)(2,1)} %tr_ref.3, bf16[8,384,256]{2,1,0:T(8,128)(2,1)} %winds.1.wind_ref, bf16[64,16,256]{2,1,0:T(8,128)(2,1)} %copy-done, bf16[64,16,256]{2,1,0:T(8,128)(2,1)} %copy-done.1, ...), custom_call_target="tpu_custom_call" | custom-call | tf_op jit(solution)/shard_map/chemistry/pallas_call | solution.py:334
  119.8 29.5 %all_to_all.5 = bf16[8,4,8,16,256]{4,3,2,1,0:T(8,128)(2,1)S(1)} all-to-all(bf16[8,4,8,16,256]{4,3,2,1,0:T(8,128)(2,1)} %get-tuple-element.23), channel_id=1, replica_groups=mesh['lat'=16,'lon'=8] {'lon'}, dimensions={0} | all-to-all | bytes 4194304 | tf_op jit(solution)/shard_map/all_to_all | solution.py:399
  149.3 0.6 convert_bitcast_fusion
  149.9 2.6 %copy.14 = f32[8,4,8,2,8,256]{5,4,0,3,2,1:T(8,128)} copy(f32[8,4,8,2,8,256]{5,4,3,2,1,0:T(8,128)S(1)} %convert_bitcast_fusion) | data formatting | bytes 8388608 | tf_op jit(solution)/shard_map/convert_element_type | solution.py:400
  (4 shorter events, 0.0 us)
Async XLA Ops:
  11.2 75.7 %collective-permute-start.3 = (bf16[256,128]{1,0:T(8,128)(2,1)}, bf16[256,128]{1,0:T(8,128)(2,1)S(1)}, u32[]{:S(2)}, u32[]{:S(2)}) collective-permute-start(bf16[256,128]{1,0:T(8,128)(2,1)} %get-tuple-element.21), channel_id=1, source_target_pairs={{0,1},{1,2},{2,3},{3,4},{4,5},{5,6},{6,7},{8,9},{9,10},{10,11},{11... | collective-permute-start | bytes 196616 | tf_op jit(solution)/shard_map/ppermute | solution.py:374
  14.8 72.2 %collective-permute-start.2 = (bf16[256,128]{1,0:T(8,128)(2,1)}, bf16[256,128]{1,0:T(8,128)(2,1)S(1)}, u32[]{:S(2)}, u32[]{:S(2)}) collective-permute-start(bf16[256,128]{1,0:T(8,128)(2,1)} %get-tuple-element.21), channel_id=1, source_target_pairs={{1,0},{2,1},{3,2},{4,3},{5,4},{6,5},{7,6},{9,8},{10,9},{11,10},{12... | collective-permute-start | bytes 196616 | tf_op jit(solution)/shard_map/ppermute | solution.py:380
  16.1 70.9 %collective-permute-start = (bf16[64,16,256]{2,1,0:T(8,128)(2,1)}, bf16[64,16,256]{2,1,0:T(8,128)(2,1)S(1)}, u32[]{:S(2)}, u32[]{:S(2)}) collective-permute-start(bf16[64,16,256]{2,1,0:T(8,128)(2,1)} %get-tuple-element.19), channel_id=1, source_target_pairs={{8,0},{16,8},{24,16},{32,24},{40,32},{48,40},{56,48},{64,56},{72,6... | collective-permute-start | bytes 1572872 | tf_op jit(solution)/shard_map/ppermute | solution.py:380
  18.9 21.0 %copy-start.4 = (s32[640]{0:T(1024)S(1)}, s32[640]{0:T(1024)}, u32[]{:S(2)}) copy-start(s32[640]{0:T(1024)} %param.12) | copy-start | bytes 7684
  18.9 21.2 %copy-start.5 = (s32[16]{0:T(128)S(1)}, s32[16]{0:T(128)}, u32[]{:S(2)}) copy-start(s32[16]{0:T(128)} %pts_ref.1) | copy-start | bytes 196
  19.0 68.0 %collective-permute-start.1 = (bf16[64,16,256]{2,1,0:T(8,128)(2,1)}, bf16[64,16,256]{2,1,0:T(8,128)(2,1)S(1)}, u32[]{:S(2)}, u32[]{:S(2)}) collective-permute-start(bf16[64,16,256]{2,1,0:T(8,128)(2,1)} %get-tuple-element.20), channel_id=1, source_target_pairs={{0,8},{8,16},{16,24},{24,32},{32,40},{40,48},{48,56},{56,64},{64,7... | collective-permute-start | bytes 1572872 | tf_op jit(solution)/shard_map/ppermute | solution.py:374
  86.9 0.6 copy-start.2
  86.9 0.6 copy-start.3
  87.0 0.8 copy-start
  87.8 0.8 copy-start.1
where the time goes:
time: 155 us; the launch traced here: 153 us
  Pallas kernels  86.4 us (56%)
  blocking collectives  29.5 us (19%)
  matrix products  14.7 us (9%)
  starting transfers between devices  14 us (9%)
  local copies, waits for them, and re-layouts  5.93 us (4%)
    pallas_call x1, Pallas kernels, winds_of(): pl.pallas_call(spectral_kernel, in_specs=[vmem, vmem, vmem, pl.BlockSpec(...  44.6 us
    pallas_call x1, Pallas kernels, chemistry(): pl.pallas_call(chem_kernel, grid_spec=pltpu.PrefetchScalarGridSpec(num_sc...  31.3 us
    all_to_all x1, blocking collectives, body(): lax.all_to_all(active, LON, split_axis=0, concat_axis=0, tiled=True)  29.5 us
    dot_general x1, matrix products, body(): lax.dot_general(spectral, legendre, (((3,), (1,)), ((2,), (0,))), preferr...  14.7 us
    pallas_call x1, Pallas kernels, edges_of(): pl.pallas_call(edge_kernel, grid=(8,), in_specs=[pl.BlockSpec((16, 8, 16,...  10.6 us
    ppermute x2, starting transfers between devices, shifted(): return lax.ppermute(value, axis, up)  9.85 us
    ppermute x2, starting transfers between devices, shifted_back(): return lax.ppermute(value, axis, up)  4.16 us
  transfers between devices with their start and end apart: 4, of which 0 were waited for; matrix products, arithmetic and copies ran while one was open for 11% of the time, Pallas kernels for 29%

commit v1 on v0

--- a/solution.py
+++ b/solution.py
@@ -13,10 +13,10 @@
 SRC = 16
 DST = 8
 MESH = pl.DeviceIdType.MESH
-COS = (0.9999999888947231, -19.739204440276147, 64.93911426452443, -85.45007790017918,
-       60.167101643628186, -25.965527386763885, 6.525643976222309)
-SIN = (6.283185302441191, -41.34170037999709, 81.60513001863838, -76.70298898514991,
-       42.02570052333535, -14.898960232258009, 3.2368479099117575)
+COS = (0.9999992006931535, -19.7389777615569, 64.92855937725766, -85.27036091136767,
+       58.78399626476764, -21.059548245283555)
+SIN = (6.283184911477688, -41.3415879428884, 81.59989458670537, -76.61384581975258,
+       41.339653019987985, -12.465497972860707)
 
 
 def waves_at(product, count, inverse):
@@ -33,10 +33,11 @@
 
 
 def spectral_kernel(
-    four_ref, rowid_ref, laneid_ref, pts_ref,
-    out_ref,
+    spec_ref, leg_ref, tr_ref, rowid_ref, laneid_ref, pts_ref,
+    out_ref, north_ref, south_ref, east_ref, west_ref,
+    spec, spread, leg, band, wide, cols, low, high, edge, empty, blank_cols,
     tall, send_a, got_a, table, phase, coef, line, turned, send_b,
-    sent_a, came_a, sent_b, came_b, own,
+    sent_a, came_a, sent_b, came_b, own, sent_h, came_h, taken, leg_in, band_in,
 ):
     g, h = lax.axis_index("lat"), lax.axis_index("lon")
     barrier = pltpu.get_barrier_semaphore()
@@ -45,8 +46,72 @@
     for d in range(1, DST):
         pl.semaphore_signal(barrier, inc=1, device_id=(g, lax.rem(h + d, DST)), device_id_type=MESH)
 
-    for k in range(2):
-        tall[k] = four_ref[:, :, 128 * k : 128 * k + 128].reshape(1920, 128).astype(jnp.float32)
+    def leg_copy(i):
+        slot = lax.rem(i, 3)
+        return pltpu.make_async_copy(leg_ref.at[pl.ds(5 * i, 5)], leg.at[slot], leg_in.at[slot])
+
+    def band_copy(i):
+        slot = lax.rem(i, 2)
+        return pltpu.make_async_copy(tr_ref.at[:, pl.ds(8 * i, 8)], band.at[slot], band_in.at[slot])
+
+    spec_copy = pltpu.make_async_copy(spec_ref, spec, taken)
+    spec_copy.start()
+    leg_copy(0).start()
+    band_copy(0).start()
+    leg_copy(1).start()
+    band_copy(1).start()
+    empty[...] = jnp.zeros_like(empty)
+    blank_cols[...] = jnp.zeros_like(blank_cols)
+    cols[...] = jnp.zeros_like(cols)
+    spec_copy.wait()
+
+    def loosen(r, carry):
+        for k in range(10):
+            spread[k, pl.ds(40 * r, 40), :] = spec[r, :, 128 * k : 128 * k + 128].astype(jnp.float32)
+        return carry
+
+    lax.fori_loop(0, 48, loosen, 0)
+    lane = lax.broadcasted_iota(jnp.int32, (256, 128), 1)
+
+    def step(i, carry):
+        slot = lax.rem(i, 3)
+
+        @pl.when(i < 6)
+        def _():
+            leg_copy(i + 2).start()
+
+        leg_copy(i).wait()
+        for w in range(5):
+            m = 5 * i + w
+            rows = [spread[k, pl.ds(m, 48, stride=40), :].astype(jnp.bfloat16) for k in range(10)]
+            value = jnp.dot(jnp.concatenate(rows, axis=1), leg[slot, w], preferred_element_type=jnp.float32)
+            for k in range(2):
+                tall[k, pl.ds(48 * m, 48), :] = value[:, 128 * k : 128 * k + 128]
+        side = lax.rem(i, 2)
+        band_copy(i).wait()
+
+        def level(l, carry):
+            at = 8 * i + l
+            x = band[side, :, l].reshape(256, 256).astype(jnp.float32)
+            for k in range(2):
+                wide[k] = x[:, 128 * k : 128 * k + 128]
+            low[at] = rows_of(wide, 0, 16, 16).astype(jnp.bfloat16)
+            high[at] = rows_of(wide, 15, 16, 16).astype(jnp.bfloat16)
+            first = pltpu.roll(x[:, :128], at, 1)
+            last = pltpu.roll(x[:, 128:], lax.rem(at + 65, 128), 1)
+            cols[...] = jnp.where(lane == at, first, jnp.where(lane == at + 64, last, cols[...]))
+            return carry
+
+        lax.fori_loop(0, 8, level, 0)
+
+        @pl.when(i < 6)
+        def _():
+            band_copy(i + 2).start()
+
+        return carry
+
+    lax.fori_loop(0, 8, step, 0)
+    edge[...] = cols[...].astype(jnp.bfloat16)
     blank = jnp.zeros((8, 128), jnp.float32)
 
     def turn(r, carry):
@@ -71,6 +136,30 @@
         copy_a(d).start()
     mine = pltpu.make_async_copy(send_a.at[g], got_a.at[g], own.at[0])
     mine.start()
+
+    def halo(k, src, dst, lat, lon):
+        return pltpu.make_async_remote_copy(
+            src_ref=src, dst_ref=dst, send_sem=sent_h.at[k], recv_sem=came_h.at[k],
+            device_id=(lat, lon), device_id_type=MESH,
+        )
+
+    to_north = halo(0, high, south_ref, lax.rem(g + 1, SRC), h)
+    to_south = halo(1, low, north_ref, lax.rem(g + SRC - 1, SRC), h)
+    to_east = halo(2, edge, west_ref, g, lax.rem(h + 1, DST))
+    to_west = halo(3, edge, east_ref, g, lax.rem(h + DST - 1, DST))
+    none_south = pltpu.make_async_copy(empty, south_ref, own.at[5])
+    none_north = pltpu.make_async_copy(empty, north_ref, own.at[6])
+    none_west = pltpu.make_async_copy(blank_cols, west_ref, own.at[7])
+    none_east = pltpu.make_async_copy(blank_cols, east_ref, own.at[8])
+    sides = (
+        (g < SRC - 1, to_north, g > 0, none_south),
+        (g > 0, to_south, g < SRC - 1, none_north),
+        (h < DST - 1, to_east, h > 0, none_west),
+        (h > 0, to_west, h < DST - 1, none_east),
+    )
+    for sends, copy, gets, fill in sides:
+        pl.when(sends)(copy.start)
+        pl.when(jnp.logical_not(gets))(fill.start)
 
     shape = (128, 128)
 
@@ -87,7 +176,9 @@
         for p in range(6):
             ids = rowid_ref[pl.ds(128 * p, 128), :]
             c, s = waves_at(ids * lane, count, inverse)
-            c1, s1 = waves_at(ids * 128.0, count, inverse)
+            c1 = jnp.broadcast_to(c[:, 64:65], shape)
+            s1 = jnp.broadcast_to(s[:, 64:65], shape)
+            c1, s1 = c1 * c1 - s1 * s1, 2.0 * c1 * s1
             table[j, pl.ds(128 * p, 128), pl.ds(0, 128)] = c.astype(jnp.bfloat16)
             table[j, pl.ds(768 + 128 * p, 128), pl.ds(0, 128)] = (-s).astype(jnp.bfloat16)
             table[j, pl.ds(128 * p, 128), pl.ds(128, 128)] = (c * c1 - s * s1).astype(jnp.bfloat16)
@@ -176,20 +267,42 @@
         return carry
 
     lax.fori_loop(0, 4, finish, 0)
-
-
-def winds_of(fourier, wave_ids, points):
+    for sends, copy, gets, fill in sides:
+        pl.when(sends)(copy.wait_send)
+        pl.when(gets)(copy.wait_recv)
+        pl.when(jnp.logical_not(gets))(fill.wait)
+
+
+def winds_of(spectral, legendre, tracers, wave_ids, points):
     ids = jnp.zeros((6, 3, 40), jnp.float32).reshape(18, 40).at[:16].set(wave_ids.reshape(16, 40).astype(jnp.float32))
     ids = jnp.pad(ids.reshape(6, 120), ((0, 0), (0, 8))).reshape(768)
     rowid = jnp.broadcast_to(ids[:, None], (768, 128))
     laneid = jnp.broadcast_to(ids[None, :], (8, 768))
     vmem = pl.BlockSpec(memory_space=pltpu.VMEM)
+    hbm = pl.BlockSpec(memory_space=pl.ANY)
     return pl.pallas_call(
         spectral_kernel,
-        in_specs=[vmem, vmem, vmem, pl.BlockSpec(memory_space=pltpu.SMEM)],
-        out_specs=pl.BlockSpec(memory_space=pl.ANY),
-        out_shape=jax.ShapeDtypeStruct((8, 384, 256), jnp.bfloat16),
+        in_specs=[hbm, hbm, hbm, vmem, vmem, pl.BlockSpec(memory_space=pltpu.SMEM)],
+        out_specs=[hbm] * 5,
+        out_shape=[
+            jax.ShapeDtypeStruct((8, 384, 256), jnp.bfloat16),
+            jax.ShapeDtypeStruct((64, 16, 256), jnp.bfloat16),
+            jax.ShapeDtypeStruct((64, 16, 256), jnp.bfloat16),
+            jax.ShapeDtypeStruct((256, 128), jnp.bfloat16),
+            jax.ShapeDtypeStruct((256, 128), jnp.bfloat16),
+        ],
         scratch_shapes=[
+            pltpu.VMEM((48, 40, 1280), jnp.bfloat16),
+            pltpu.VMEM((10, 1920, 128), jnp.float32),
+            pltpu.VMEM((3, 5, 1280, 256), jnp.bfloat16),
+            pltpu.VMEM((2, 16, 8, 16, 256), jnp.bfloat16),
+            pltpu.VMEM((2, 256, 128), jnp.float32),
+            pltpu.VMEM((256, 128), jnp.float32),
+            pltpu.VMEM((64, 16, 256), jnp.bfloat16),
+            pltpu.VMEM((64, 16, 256), jnp.bfloat16),
+            pltpu.VMEM((256, 128), jnp.bfloat16),
+            pltpu.VMEM((64, 16, 256), jnp.bfloat16),
+            pltpu.VMEM((256, 128), jnp.bfloat16),
             pltpu.VMEM((2, 1920, 128), jnp.float32),
             pltpu.VMEM((16, 16, 16, 128), jnp.bfloat16),
             pltpu.VMEM((16, 16, 16, 128), jnp.bfloat16),
@@ -203,64 +316,22 @@
             pltpu.SemaphoreType.DMA((16,)),
             pltpu.SemaphoreType.DMA((4, 8)),
             pltpu.SemaphoreType.DMA((4, 8)),
-            pltpu.SemaphoreType.DMA((5,)),
+            pltpu.SemaphoreType.DMA((9,)),
+            pltpu.SemaphoreType.DMA((4,)),
+            pltpu.SemaphoreType.DMA((4,)),
+            pltpu.SemaphoreType.DMA,
+            pltpu.SemaphoreType.DMA((3,)),
+            pltpu.SemaphoreType.DMA((2,)),
         ],
         compiler_params=pltpu.CompilerParams(
             collective_id=0, has_side_effects=True, vmem_limit_bytes=60 * 1024 * 1024
         ),
         name="winds",
-    )(fourier, rowid, laneid, points)
+    )(spectral, legendre, tracers, rowid, laneid, points)
 
 
 def rows_of(ref, start, size, stride):
     return jnp.concatenate([ref[k, pl.ds(start, size, stride=stride), :] for k in range(2)], axis=1)
-
-
-def edge_kernel(tr_ref, low_ref, high_ref, col_ref, wide, acc):
-    h = pl.program_id(0)
-    lane = lax.broadcasted_iota(jnp.int32, (256, 128), 1)
-
-    @pl.when(h == 0)
-    def _():
-        acc[...] = jnp.zeros_like(acc)
-
-    def level(l, carry):
-        x = tr_ref[:, l].reshape(256, 256).astype(jnp.float32)
-        for k in range(2):
-            wide[k] = x[:, 128 * k : 128 * k + 128]
-        low_ref[l] = rows_of(wide, 0, 16, 16).astype(jnp.bfloat16)
-        high_ref[l] = rows_of(wide, 15, 16, 16).astype(jnp.bfloat16)
-        at = h * 8 + l
-        first = pltpu.roll(x[:, :128], at, 1)
-        last = pltpu.roll(x[:, 128:], lax.rem(at + 65, 128), 1)
-        acc[...] = jnp.where(lane == at, first, jnp.where(lane == at + 64, last, acc[...]))
-        return carry
-
-    lax.fori_loop(0, 8, level, 0)
-
-    @pl.when(h == pl.num_programs(0) - 1)
-    def _():
-        col_ref[...] = acc[...].astype(jnp.bfloat16)
-
-
-def edges_of(tracers):
-    return pl.pallas_call(
-        edge_kernel,
-        grid=(8,),
-        in_specs=[pl.BlockSpec((16, 8, 16, 256), lambda h: (0, h, 0, 0))],
-        out_specs=[
-            pl.BlockSpec((8, 16, 256), lambda h: (h, 0, 0)),
-            pl.BlockSpec((8, 16, 256), lambda h: (h, 0, 0)),
-            pl.BlockSpec((256, 128), lambda h: (0, 0)),
-        ],
-        out_shape=[
-            jax.ShapeDtypeStruct((64, 16, 256), jnp.bfloat16),
-            jax.ShapeDtypeStruct((64, 16, 256), jnp.bfloat16),
-            jax.ShapeDtypeStruct((256, 128), jnp.bfloat16),
-        ],
-        scratch_shapes=[pltpu.VMEM((2, 256, 128), jnp.float32), pltpu.VMEM((256, 128), jnp.float32)],
-        name="edges",
-    )(tracers)
 
 
 def chem_kernel(
@@ -368,29 +439,10 @@
     )(ids, tracers, winds, north, south, east, west, mask, base, temp)
 
 
-def shifted(value, axis):
-    size = lax.axis_size(axis)
-    up = [(i, (i + 1) % size) for i in range(size - 1)]
-    return lax.ppermute(value, axis, up)
-
-
-def shifted_back(value, axis):
-    size = lax.axis_size(axis)
-    up = [((i + 1) % size, i) for i in range(size - 1)]
-    return lax.ppermute(value, axis, up)
-
-
 def body(spectral, legendre, wave_ids, points, tracers, react_base, react_temp, active_ids):
-    low, high, cols = edges_of(tracers)
-    south = shifted(high, "lat")
-    north = shifted_back(low, "lat")
-    west = shifted(cols, LON)
-    east = shifted_back(cols, LON)
-    fourier = lax.dot_general(
-        spectral, legendre, (((3,), (1,)), ((2,), (0,))), preferred_element_type=jnp.float32
+    winds, north, south, east, west = winds_of(
+        spectral.reshape(48, 40, 1280), legendre, tracers, wave_ids, points
     )
-    fourier = fourier.astype(jnp.bfloat16)
-    winds = winds_of(fourier.reshape(40, 48, 256), wave_ids, points)
     columns = lax.axis_index("lon") * 256 + jnp.arange(256)
     mask = (columns[None, :] < points[:, None]).astype(jnp.float32)
     fresh, active = chemistry(

time: 155 us -> 132 us (0.85); the launches traced: 153 us -> 132 us
  matrix products: 14.7 us -> 0 us
  starting transfers between devices: 14 us -> 0 us
  Pallas kernels: 86.4 us -> 97 us
  blocking collectives: 29.5 us -> 27.4 us
  local copies, waits for them, and re-layouts: 5.93 us -> 4.33 us
    dot_general x1 -> x0, matrix products: 14.7 us -> none  [body(): lax.dot_general(spectral, legendre, (((3,), (1,)), ((2,), (0,))), preferr...]
    ppermute x4 -> x0, starting transfers between devices: 14 us -> none  [the longest x2 9.85 us: shifted(): return lax.ppermute(value, axis, up)]
    pallas_call x2 -> x1, Pallas kernels: 55.2 us -> 65.7 us  [winds_of(): pl.pallas_call(spectral_kernel, in_specs=[hbm, hbm, hbm, vmem, vmem, pl.B...]
    all_to_all x1, blocking collectives: 29.5 us -> 27.4 us  [body(): lax.all_to_all(active, LON, split_axis=0, concat_axis=0, tiled=True)]
    unnamed x12 -> x0, local copies, waits for them, and re-layouts: 1.59 us -> none
  transfers between devices with their start and end apart: 4 -> 0, of which waited for: 0 -> 0; matrix products, arithmetic and copies ran while one was open for 11% -> 0% of each run, Pallas kernels for 29% -> 0%
where the time goes in v1:
time: 132 us
  Pallas kernels  97 us (73%)
  blocking collectives  27.4 us (21%)
  local copies, waits for them, and re-layouts  4.33 us (3%)
  other arithmetic  2.59 us (2%)
    pallas_call x1, Pallas kernels, winds_of(): pl.pallas_call(spectral_kernel, in_specs=[hbm, hbm, hbm, vmem, vmem, pl.B...  65.7 us
    pallas_call x1, Pallas kernels, chemistry(): pl.pallas_call(chem_kernel, grid_spec=pltpu.PrefetchScalarGridSpec(num_sc...  31.2 us
    all_to_all x1, blocking collectives, body(): lax.all_to_all(active, LON, split_axis=0, concat_axis=0, tiled=True)  27.4 us
    convert_element_type x1, local copies, waits for them, and re-layouts, body(): jnp.transpose(active, (1, 2, 3, 0, 4)).reshape(4, 8, 16, 2048)  2.65 us

profile of v1, /device:TPU:25, one launch (start us, length us, event | category | flops | bytes accessed | tf_op | source)
XLA Modules:
  0.0 131.9 jit_solution(8507606405634205491)
XLA Ops:
  0.6 0.7 convert_element_type.20
  1.3 0.1 convert_element_type.21
  1.4 0.1 reshape.50
  1.5 1.3 %compare_convert_fusion.mask_ref = f32[16,256]{1,0:T(8,128)} fusion(s32[256]{0:T(256)S(1)} %iota_add_fusion, s32[16]{0:T(128)} %pts_ref.1), kind=kLoop, calls=%fused_computation.1 | loop fusion | flops 8192 | bytes 17472 | tf_op jit(solution)/shard_map/convert_element_type | solution.py:447
  2.8 0.6 broadcast_in_dim.16.laneid_ref
  3.5 0.9 broadcast_in_dim.7.rowid_ref
  4.4 65.7 %winds.1 = (bf16[8,384,256]{2,1,0:T(8,128)(2,1)}, bf16[64,16,256]{2,1,0:T(8,128)(2,1)}, bf16[64,16,256]{2,1,0:T(8,128)(2,1)}, bf16[256,128]{1,0:T(8,128)(2,1)}, bf16[256,128]{1,0:T(8,128)(2,1)}) custom-call(bf16[48,40,1280]{2,1,0:T(8,128)(2,1)} %bitcast.7, bf16[40,1280,256]{2,1,0:T(8,128)(2,1)} %leg_ref.1, bf16[16,64,16,256]{3,2,1,0:T(8,128)(2,1)} %tr_ref.3, ...), custom_call_target="tpu_custom_call" | custom-call | tf_op jit(solution)/shard_map/winds/pallas_call | solution.py:283
  70.1 31.2 %chemistry.1 = (bf16[16,64,16,256]{3,2,1,0:T(8,128)(2,1)}, bf16[8,4,8,16,256]{4,3,2,1,0:T(8,128)(2,1)}) custom-call(s32[4]{0:T(128)} %ids_ref.1, bf16[16,64,16,256]{3,2,1,0:T(8,128)(2,1)} %tr_ref.3, bf16[8,384,256]{2,1,0:T(8,128)(2,1)} %get-tuple-element.21.wind_ref, bf16[64,16,256]{2,1,0:T(8,128)(2,1)} %get-tuple-element.22.north_ref, ...), custom_call_target="tpu_custom_call" | custom-call | tf_op jit(solution)/shard_map/chemistry/pallas_call | solution.py:405
  101.3 27.4 %all_to_all.5 = bf16[8,4,8,16,256]{4,3,2,1,0:T(8,128)(2,1)S(1)} all-to-all(bf16[8,4,8,16,256]{4,3,2,1,0:T(8,128)(2,1)} %get-tuple-element.27), channel_id=1, replica_groups=mesh['lat'=16,'lon'=8] {'lon'}, dimensions={0} | all-to-all | bytes 4194304 | tf_op jit(solution)/shard_map/all_to_all | solution.py:451
  128.7 0.6 convert_bitcast_fusion
  129.3 2.6 %copy.11 = f32[8,4,8,2,8,256]{5,4,0,3,2,1:T(8,128)} copy(f32[8,4,8,2,8,256]{5,4,3,2,1,0:T(8,128)S(1)} %convert_bitcast_fusion) | data formatting | bytes 8388608 | tf_op jit(solution)/shard_map/convert_element_type | solution.py:452
  (3 shorter events, 0.0 us)

commit v2 on v1

--- a/solution.py
+++ b/solution.py
@@ -11,6 +11,8 @@
 
 
 SRC = 16
+UNROLL = 4
+CHUNK = 8
 DST = 8
 MESH = pl.DeviceIdType.MESH
 COS = (0.9999992006931535, -19.7389777615569, 64.92855937725766, -85.27036091136767,
@@ -335,13 +337,28 @@
 
 
 def chem_kernel(
-    ids_ref, tr_ref, wind_ref, north_ref, south_ref, east_ref, west_ref, mask_ref, base_ref, temp_ref,
-    out_ref, act_ref, wide, east, west, mix, moved, moved_b,
+    ids_ref, tr_ref, wind_ref, north_ref, south_ref, east_ref, west_ref, mask_ref, base_ref, temp_ref, *rest
 ):
-    h = pl.program_id(0)
-
-    @pl.when(h == 0)
+    out_ref, got_ref, wide, east, west, mix, *kept = rest
+    towers, moved, moved_b = kept[:2], kept[2:4], kept[4:6]
+    chosen, sent, came, own = kept[6:]
+    step = pl.program_id(0)
+    g, tile = lax.axis_index("lat"), lax.axis_index("lon")
+    h = lax.rem(tile + 1 + step, DST)
+    levels = out_ref.shape[1]
+    barrier = pltpu.get_barrier_semaphore()
+
+    def send(d):
+        to = lax.rem(tile + d, DST)
+        return pltpu.make_async_remote_copy(
+            src_ref=chosen.at[to], dst_ref=got_ref.at[tile], send_sem=sent.at[d], recv_sem=came.at[d],
+            device_id=(g, to), device_id_type=MESH,
+        )
+
+    @pl.when(step == 0)
     def _():
+        for d in range(1, DST):
+            pl.semaphore_signal(barrier, inc=1, device_id=(g, lax.rem(tile + d, DST)), device_id_type=MESH)
         east[...] = east_ref[...].astype(jnp.float32)
         west[...] = west_ref[...].astype(jnp.float32)
         row = lax.broadcasted_iota(jnp.int32, (256, 16), 0)
@@ -355,86 +372,130 @@
             full = lax.dot_general(
                 rows.astype(jnp.bfloat16), spread, (((1,), (1,)), ((), ())), preferred_element_type=jnp.float32
             )
-            mix[pl.ds(256 * k, 256), :] = jnp.where(same, full, 0.0).astype(jnp.bfloat16)
+            full = jnp.where(same, full, 0.0).astype(jnp.bfloat16)
+            for c in range(0, 16, CHUNK):
+                mix[pl.ds(32 * c + 16 * CHUNK * k, 16 * CHUNK), :] = full[16 * c : 16 * (c + CHUNK)]
 
     for k in range(2):
         wide[k] = wind_ref[0, :, 128 * k : 128 * k + 128].astype(jnp.float32)
     lane = lax.broadcasted_iota(jnp.int32, (16, 128), 1)
-    row = lax.broadcasted_iota(jnp.int32, (16, 256), 0)
-    lane_low, lane_high = lane == 0, lane == 127
-    row_low, row_high = row == 0, row == 15
     mask = mask_ref[...]
 
-    def level(l, carry):
+    def advect(l, kept, kept_b, tower):
         at = h * 8 + l
-        u = 0.1 * rows_of(wide, l, 16, 24)
-        v = 0.1 * rows_of(wide, 8 + l, 16, 24)
-        temper = rows_of(wide, 16 + l, 16, 24)
-        east_w, west_w = 0.05 - u, 0.05 + u
-        north_w, south_w = 0.05 - v, 0.05 + v
-        north = north_ref[l].astype(jnp.float32)
-        south = south_ref[l].astype(jnp.float32)
+        local = l
+        u = 0.1 * rows_of(wide, local, 16, 24)
+        v = 0.1 * rows_of(wide, 8 + local, 16, 24)
+        east_w, west_w = (0.05 - u) * mask, (0.05 + u) * mask
+        north_w, south_w = (0.05 - v) * mask, (0.05 + v) * mask
+        own_w = 0.8 * mask
+        for k in range(2):
+            half = slice(128 * k, 128 * k + 128)
+            tower[k, pl.ds(0, 16, stride=36), :] = south_ref[l, :, half].astype(jnp.float32)
+            tower[k, pl.ds(34, 16, stride=36), :] = north_ref[l, :, half].astype(jnp.float32)
         for t in range(16):
             x = tr_ref[t, l].astype(jnp.float32)
             xl, xr = x[:, :128], x[:, 128:]
+            for k, part_x in enumerate((xl, xr)):
+                tower[k, pl.ds(36 * t + 2, 16, stride=2), :] = part_x
             he = pltpu.roll(east[pl.ds(16 * t, 16), :], 127 - at, 1)
             hw = pltpu.roll(west[pl.ds(16 * t, 16), :], 64 - at, 1)
             el, er = pltpu.roll(xl, 127, 1), pltpu.roll(xr, 127, 1)
             wl, wr = pltpu.roll(xl, 1, 1), pltpu.roll(xr, 1, 1)
-            xe = jnp.concatenate([jnp.where(lane_high, er, el), jnp.where(lane_high, he, er)], axis=1)
-            xw = jnp.concatenate([jnp.where(lane_low, hw, wl), jnp.where(lane_low, wl, wr)], axis=1)
-            xn = jnp.where(row_high, north[t : t + 1, :], pltpu.roll(x, 15, 0))
-            xs = jnp.where(row_low, south[t : t + 1, :], pltpu.roll(x, 1, 0))
-            q = 0.8 * x + east_w * xe + west_w * xw + north_w * xn + south_w * xs
-            moved[t] = q
-            moved_b[pl.ds(16 * t, 16), :] = q.astype(jnp.bfloat16)
-        y = jnp.dot(mix[...], moved_b[...], preferred_element_type=jnp.float32)
-        for t in range(16):
-            q = (moved[t] + y[16 * t : 16 * t + 16] + temper * y[256 + 16 * t : 272 + 16 * t]) * mask
-            moved[t] = q
-            out_ref[t, l] = q.astype(jnp.bfloat16)
+            xe = jnp.concatenate([jnp.where(lane == 127, er, el), jnp.where(lane == 127, he, er)], axis=1)
+            xw = jnp.concatenate([jnp.where(lane == 0, hw, wl), jnp.where(lane == 0, wl, wr)], axis=1)
+            xn = rows_of(tower, 36 * t + 4, 16, 2)
+            xs = rows_of(tower, 36 * t, 16, 2)
+            q = own_w * x + east_w * xe + west_w * xw + north_w * xn + south_w * xs
+            kept[t] = q
+            kept_b[pl.ds(16 * t, 16), :] = q.astype(jnp.bfloat16)
+
+    def settle(l, kept, kept_b):
+        temper = rows_of(wide, 16 + l, 16, 24)
+        for c in range(0, 16, CHUNK):
+            y = jnp.dot(mix[pl.ds(32 * c, 32 * CHUNK), :], kept_b[...], preferred_element_type=jnp.float32)
+            for t in range(CHUNK):
+                base, heat = y[16 * t : 16 * t + 16], y[16 * (CHUNK + t) : 16 * (CHUNK + t) + 16]
+                q = kept[c + t] + base + temper * heat
+                kept[c + t] = q
+                out_ref[c + t, l] = q.astype(jnp.bfloat16)
         for a in range(4):
-            act_ref[0, a, l] = moved[ids_ref[a]].astype(jnp.bfloat16)
-        return carry
-
-    lax.fori_loop(0, 8, level, 0)
+            chosen[h, a, l] = kept[ids_ref[a]].astype(jnp.bfloat16)
+
+    def several(i, carry):
+        pend = None
+        for k in range(UNROLL):
+            l = UNROLL * i + k
+            now = (l, moved[k % 2], moved_b[k % 2])
+            advect(*now, towers[k % 2])
+            if pend is not None:
+                settle(*pend)
+            pend = now
+        settle(*pend)
+        return carry
+
+    lax.fori_loop(0, levels // UNROLL, several, 0)
+
+    @pl.when(step == 0)
+    def _():
+        pl.semaphore_wait(barrier, DST - 1)
+
+    @pl.when(step < DST - 1)
+    def _():
+        send(step + 1).start()
+
+    @pl.when(step == DST - 1)
+    def _():
+        mine = pltpu.make_async_copy(chosen.at[tile], got_ref.at[tile], own)
+        mine.start()
+        mine.wait()
+        for d in range(1, DST):
+            send(d).wait()
 
 
 def chemistry(tracers, winds, north, south, east, west, mask, base, temp, ids):
-    whole = lambda h, i: (0, 0)
+    whole = lambda s, i: (0, 0)
+    source = lambda s: lax.rem(lax.axis_index("lon") + 1 + s, DST)
+    hbm = pl.BlockSpec(memory_space=pl.ANY)
     return pl.pallas_call(
         chem_kernel,
         grid_spec=pltpu.PrefetchScalarGridSpec(
             num_scalar_prefetch=1,
             grid=(8,),
             in_specs=[
-                pl.BlockSpec((16, 8, 16, 256), lambda h, i: (0, h, 0, 0)),
-                pl.BlockSpec((1, 384, 256), lambda h, i: (h, 0, 0)),
-                pl.BlockSpec((8, 16, 256), lambda h, i: (h, 0, 0)),
-                pl.BlockSpec((8, 16, 256), lambda h, i: (h, 0, 0)),
+                pl.BlockSpec((16, 8, 16, 256), lambda s, i: (0, source(s), 0, 0)),
+                pl.BlockSpec((1, 384, 256), lambda s, i: (source(s), 0, 0)),
+                pl.BlockSpec((8, 16, 256), lambda s, i: (source(s), 0, 0)),
+                pl.BlockSpec((8, 16, 256), lambda s, i: (source(s), 0, 0)),
                 pl.BlockSpec((256, 128), whole),
                 pl.BlockSpec((256, 128), whole),
                 pl.BlockSpec((16, 256), whole),
                 pl.BlockSpec((16, 16), whole),
                 pl.BlockSpec((16, 16), whole),
             ],
-            out_specs=[
-                pl.BlockSpec((16, 8, 16, 256), lambda h, i: (0, h, 0, 0)),
-                pl.BlockSpec((1, 4, 8, 16, 256), lambda h, i: (h, 0, 0, 0, 0)),
-            ],
+            out_specs=[pl.BlockSpec((16, 8, 16, 256), lambda s, i: (0, source(s), 0, 0)), hbm],
             scratch_shapes=[
                 pltpu.VMEM((2, 384, 128), jnp.float32),
                 pltpu.VMEM((256, 128), jnp.float32),
                 pltpu.VMEM((256, 128), jnp.float32),
                 pltpu.VMEM((512, 256), jnp.bfloat16),
+                pltpu.VMEM((2, 576, 128), jnp.float32),
+                pltpu.VMEM((2, 576, 128), jnp.float32),
+                pltpu.VMEM((16, 16, 256), jnp.float32),
                 pltpu.VMEM((16, 16, 256), jnp.float32),
                 pltpu.VMEM((256, 256), jnp.bfloat16),
+                pltpu.VMEM((256, 256), jnp.bfloat16),
+                pltpu.VMEM((8, 4, 8, 16, 256), jnp.bfloat16),
+                pltpu.SemaphoreType.DMA((8,)),
+                pltpu.SemaphoreType.DMA((8,)),
+                pltpu.SemaphoreType.DMA,
             ],
         ),
         out_shape=[
             jax.ShapeDtypeStruct((16, 64, 16, 256), jnp.bfloat16),
             jax.ShapeDtypeStruct((8, 4, 8, 16, 256), jnp.bfloat16),
         ],
+        compiler_params=pltpu.CompilerParams(collective_id=1, has_side_effects=True),
         name="chemistry",
     )(ids, tracers, winds, north, south, east, west, mask, base, temp)
 
@@ -448,7 +509,6 @@
     fresh, active = chemistry(
         tracers, winds, north, south, east, west, mask, react_base, react_temp, active_ids
     )
-    active = lax.all_to_all(active, LON, split_axis=0, concat_axis=0, tiled=True)
     active = jnp.transpose(active, (1, 2, 3, 0, 4)).reshape(4, 8, 16, 2048).astype(jnp.float32)
     return (fresh, active)
 

time: 132 us -> 118 us (0.89)
  the two profiles are of different devices: /device:TPU:25 before, /device:TPU:32 now
where the time goes in v2:
time: 118 us
  Pallas kernels  101 us (86%)
  local copies, waits for them, and re-layouts  11.8 us (10%)
  other arithmetic  4.18 us (4%)
    pallas_call x1, Pallas kernels, winds_of(): pl.pallas_call(spectral_kernel, in_specs=[hbm, hbm, hbm, vmem, vmem, pl.B...  60.8 us
    pallas_call x1, Pallas kernels, chemistry(): pl.pallas_call(chem_kernel, grid_spec=pltpu.PrefetchScalarGridSpec(num_sc...  40.5 us
    unnamed x1, local copies, waits for them, and re-layouts  7.52 us
    convert_element_type x1, local copies, waits for them, and re-layouts, body(): jnp.transpose(active, (1, 2, 3, 0, 4)).reshape(4, 8, 16, 2048)  2.65 us

profile of v2, /device:TPU:32, one launch (start us, length us, event | category | flops | bytes accessed | tf_op | source)
XLA Modules:
  0.0 118.1 jit_solution(15771891452811097982)
XLA Ops:
  0.6 0.7 convert_element_type.20
  1.3 0.1 convert_element_type.21
  1.4 0.1 reshape.50
  1.5 1.3 %compare_convert_fusion.mask_ref = f32[16,256]{1,0:T(8,128)} fusion(s32[256]{0:T(256)S(1)} %iota_add_fusion, s32[16]{0:T(128)} %pts_ref.1), kind=kLoop, calls=%fused_computation.1 | loop fusion | flops 8192 | bytes 17472 | tf_op jit(solution)/shard_map/convert_element_type | solution.py:508
  2.8 0.6 broadcast_in_dim.16.laneid_ref
  3.5 0.9 broadcast_in_dim.7.rowid_ref
  4.4 60.8 %winds.1 = (bf16[8,384,256]{2,1,0:T(8,128)(2,1)}, bf16[64,16,256]{2,1,0:T(8,128)(2,1)}, bf16[64,16,256]{2,1,0:T(8,128)(2,1)}, bf16[256,128]{1,0:T(8,128)(2,1)}, bf16[256,128]{1,0:T(8,128)(2,1)}) custom-call(bf16[48,40,1280]{2,1,0:T(8,128)(2,1)} %bitcast.7, bf16[40,1280,256]{2,1,0:T(8,128)(2,1)} %leg_ref.1, bf16[16,64,16,256]{3,2,1,0:T(8,128)(2,1)} %tr_ref.3, ...), custom_call_target="tpu_custom_call" | custom-call | tf_op jit(solution)/shard_map/winds/pallas_call | solution.py:285
  65.2 40.5 %chemistry.1 = (bf16[16,64,16,256]{3,2,1,0:T(8,128)(2,1)}, bf16[8,4,8,16,256]{4,3,2,1,0:T(8,128)(2,1)}) custom-call(s32[4]{0:T(128)} %ids_ref.1, bf16[16,64,16,256]{3,2,1,0:T(8,128)(2,1)} %tr_ref.3, bf16[8,384,256]{2,1,0:T(8,128)(2,1)} %get-tuple-element.21.wind_ref, bf16[64,16,256]{2,1,0:T(8,128)(2,1)} %get-tuple-element.22.north_ref, ...), custom_call_target="tpu_custom_call" | custom-call | tf_op jit(solution)/shard_map/chemistry/pallas_call | solution.py:460
  105.8 2.2 %convert_bitcast_fusion = f32[8,4,8,2,8,256]{5,4,3,2,1,0:T(8,128)S(1)} fusion(bf16[8,4,8,16,256]{4,3,2,1,0:T(8,128)(2,1)} %get-tuple-element.27), kind=kLoop, calls=%fused_computation | loop fusion | flops 1048576 | bytes 6291456
  107.9 2.6 %copy.11 = f32[8,4,8,2,8,256]{5,4,0,3,2,1:T(8,128)} copy(f32[8,4,8,2,8,256]{5,4,3,2,1,0:T(8,128)S(1)} %convert_bitcast_fusion) | data formatting | bytes 8388608 | tf_op jit(solution)/shard_map/convert_element_type | solution.py:512
  110.6 7.5 %copy.13 = bf16[16,64,16,256]{3,2,1,0:T(8,128)(2,1)} copy(bf16[16,64,16,256]{3,2,1,0:T(8,128)(2,1)} %get-tuple-element.30) | data formatting | bytes 16777216
  (3 shorter events, 0.0 us)

commit v3 on v2

--- a/solution.py
+++ b/solution.py
@@ -15,10 +15,31 @@
 CHUNK = 8
 DST = 8
 MESH = pl.DeviceIdType.MESH
+TILES = ((2, 1), (2, 0), (1, 1), (3, 0), (3, 1), (1, 0), (0, 1))
+BANDS = (
+    (1, 2, 0), (1, 2, 1), (0, 1, 0), (1, 0, 0), (0, 3, 1), (1, 1, 0), (0, 2, 0), (1, 3, 1),
+    (0, 1, 1), (1, 0, 1), (0, 3, 0), (1, 1, 1), (0, 2, 1), (1, 3, 0), (0, 0, 1),
+)
 COS = (0.9999992006931535, -19.7389777615569, 64.92855937725766, -85.27036091136767,
        58.78399626476764, -21.059548245283555)
 SIN = (6.283184911477688, -41.3415879428884, 81.59989458670537, -76.61384581975258,
        41.339653019987985, -12.465497972860707)
+
+
+def tile_at(h, dx, dz, back=False):
+    dx = (4 - dx) % 4 if back else dx
+    return lax.rem(h // 2 + dx, 4) * 2 + lax.rem(lax.rem(h, 2) + dz, 2)
+
+
+def band_at(g, dz, dy, dc):
+    high = lax.rem(g // 8 + dz, 2)
+    return high * 8 + lax.rem(lax.rem(g // 2, 4) + dy, 4) * 2 + lax.rem(lax.rem(g, 2) + dc, 2)
+
+
+def tile_of_step(h, s):
+    power = (1 + 3 * lax.rem(s, 2)) * (1 + 15 * lax.rem(s // 2, 2)) * (1 + 255 * (s // 4))
+    code = sum(dx * 4**k for k, (dx, dz) in enumerate(TILES))
+    return lax.rem(h // 2 + lax.rem(code // power, 4), 4) * 2 + lax.rem(lax.rem(h, 2) + 1 + s, 2)
 
 
 def waves_at(product, count, inverse):
@@ -35,10 +56,10 @@
 
 
 def spectral_kernel(
-    spec_ref, leg_ref, tr_ref, rowid_ref, laneid_ref, pts_ref,
+    spec_ref, leg_ref, tr_ref, ids_ref, pts_ref,
     out_ref, north_ref, south_ref, east_ref, west_ref,
-    spec, spread, leg, band, wide, cols, low, high, edge, empty, blank_cols,
-    tall, send_a, got_a, table, phase, coef, line, turned, send_b,
+    spec, spread, leg, band, wide_0, wide_1, wide_2, wide_3, cols, low, high, edge, empty, blank_cols,
+    rowid, laneid, tall, send_a, got_a, table, phase, coef, line, turned, send_b,
     sent_a, came_a, sent_b, came_b, own, sent_h, came_h, taken, leg_in, band_in,
 ):
     g, h = lax.axis_index("lat"), lax.axis_index("lon")
@@ -48,6 +69,8 @@
     for d in range(1, DST):
         pl.semaphore_signal(barrier, inc=1, device_id=(g, lax.rem(h + d, DST)), device_id_type=MESH)
 
+    wide = (wide_0, wide_1, wide_2, wide_3)
+
     def leg_copy(i):
         slot = lax.rem(i, 3)
         return pltpu.make_async_copy(leg_ref.at[pl.ds(5 * i, 5)], leg.at[slot], leg_in.at[slot])
@@ -62,49 +85,84 @@
     band_copy(0).start()
     leg_copy(1).start()
     band_copy(1).start()
+    leg_copy(2).start()
+    for p in range(6):
+        ids = jnp.broadcast_to(ids_ref[p : p + 1, :], (128, 128)).astype(jnp.float32)
+        laneid[:, 128 * p : 128 * p + 128] = ids[:8]
+        rowid[128 * p : 128 * p + 128, :] = ids.T
     empty[...] = jnp.zeros_like(empty)
     blank_cols[...] = jnp.zeros_like(blank_cols)
     cols[...] = jnp.zeros_like(cols)
     spec_copy.wait()
 
-    def loosen(r, carry):
-        for k in range(10):
-            spread[k, pl.ds(40 * r, 40), :] = spec[r, :, 128 * k : 128 * k + 128].astype(jnp.float32)
-        return carry
-
-    lax.fori_loop(0, 48, loosen, 0)
+    def loosen(i, carry):
+        for r in range(4):
+            for k in range(10):
+                part = spec[4 * i + r, :, 128 * k : 128 * k + 128]
+                spread[k, pl.ds(160 * i + 40 * r, 40), :] = part.astype(jnp.float32)
+        return carry
+
+    lax.fori_loop(0, 12, loosen, 0)
     lane = lax.broadcasted_iota(jnp.int32, (256, 128), 1)
+
+    shape = (128, 128)
+
+    def tables(j, carry):
+        count = jnp.full((1, 1), pts_ref[j], jnp.int32).astype(jnp.float32)
+        inverse = 1.0 / count
+        far = lax.broadcasted_iota(jnp.int32, (8, 128), 0).astype(jnp.float32) * 256.0
+        lane = lax.broadcasted_iota(jnp.int32, shape, 1).astype(jnp.float32)
+        for p in range(6):
+            ids = laneid[:, pl.ds(128 * p, 128)]
+            c, s = waves_at(ids * far, count, inverse)
+            phase[j, 0, p] = c
+            phase[j, 1, p] = s
+        for p in range(6):
+            ids = rowid[pl.ds(128 * p, 128), :]
+            c, s = waves_at(ids * lane, count, inverse)
+            c1 = jnp.broadcast_to(c[:, 64:65], shape)
+            s1 = jnp.broadcast_to(s[:, 64:65], shape)
+            c1, s1 = c1 * c1 - s1 * s1, 2.0 * c1 * s1
+            table[j, pl.ds(128 * p, 128), pl.ds(0, 128)] = c.astype(jnp.bfloat16)
+            table[j, pl.ds(768 + 128 * p, 128), pl.ds(0, 128)] = (-s).astype(jnp.bfloat16)
+            table[j, pl.ds(128 * p, 128), pl.ds(128, 128)] = (c * c1 - s * s1).astype(jnp.bfloat16)
+            table[j, pl.ds(768 + 128 * p, 128), pl.ds(128, 128)] = (-(s * c1 + c * s1)).astype(jnp.bfloat16)
+        return carry
 
     def step(i, carry):
         slot = lax.rem(i, 3)
-
-        @pl.when(i < 6)
-        def _():
-            leg_copy(i + 2).start()
-
         leg_copy(i).wait()
+        tables(i, 0)
         for w in range(5):
             m = 5 * i + w
             rows = [spread[k, pl.ds(m, 48, stride=40), :].astype(jnp.bfloat16) for k in range(10)]
             value = jnp.dot(jnp.concatenate(rows, axis=1), leg[slot, w], preferred_element_type=jnp.float32)
             for k in range(2):
                 tall[k, pl.ds(48 * m, 48), :] = value[:, 128 * k : 128 * k + 128]
+
+        @pl.when(i < 5)
+        def _():
+            leg_copy(i + 3).start()
+
         side = lax.rem(i, 2)
         band_copy(i).wait()
 
         def level(l, carry):
-            at = 8 * i + l
-            x = band[side, :, l].reshape(256, 256).astype(jnp.float32)
-            for k in range(2):
-                wide[k] = x[:, 128 * k : 128 * k + 128]
-            low[at] = rows_of(wide, 0, 16, 16).astype(jnp.bfloat16)
-            high[at] = rows_of(wide, 15, 16, 16).astype(jnp.bfloat16)
-            first = pltpu.roll(x[:, :128], at, 1)
-            last = pltpu.roll(x[:, 128:], lax.rem(at + 65, 128), 1)
-            cols[...] = jnp.where(lane == at, first, jnp.where(lane == at + 64, last, cols[...]))
+            kept = cols[...]
+            for n in range(4):
+                at = 8 * i + 4 * l + n
+                x = band[side, :, 4 * l + n].reshape(256, 256).astype(jnp.float32)
+                for k in range(2):
+                    wide[n][k] = x[:, 128 * k : 128 * k + 128]
+                low[at] = rows_of(wide[n], 0, 16, 16).astype(jnp.bfloat16)
+                high[at] = rows_of(wide[n], 15, 16, 16).astype(jnp.bfloat16)
+                first = pltpu.roll(x[:, :128], at, 1)
+                last = pltpu.roll(x[:, 128:], lax.rem(at + 65, 128), 1)
+                kept = jnp.where(lane == at, first, jnp.where(lane == at + 64, last, kept))
+            cols[...] = kept
             return carry
 
-        lax.fori_loop(0, 8, level, 0)
+        lax.fori_loop(0, 2, level, 0)
 
         @pl.when(i < 6)
         def _():
@@ -128,7 +186,7 @@
     pl.semaphore_wait(barrier, SRC + DST - 2)
 
     def copy_a(d):
-        to = lax.rem(g + d, SRC)
+        to = band_at(g, *BANDS[d - 1])
         return pltpu.make_async_remote_copy(
             src_ref=send_a.at[to], dst_ref=got_a.at[g], send_sem=sent_a.at[d], recv_sem=came_a.at[d],
             device_id=(to, h), device_id_type=MESH,
@@ -163,31 +221,7 @@
         pl.when(sends)(copy.start)
         pl.when(jnp.logical_not(gets))(fill.start)
 
-    shape = (128, 128)
-
-    def tables(j, carry):
-        count = jnp.full((1, 1), pts_ref[j], jnp.int32).astype(jnp.float32)
-        inverse = 1.0 / count
-        far = lax.broadcasted_iota(jnp.int32, (8, 128), 0).astype(jnp.float32) * 256.0
-        lane = lax.broadcasted_iota(jnp.int32, shape, 1).astype(jnp.float32)
-        for p in range(6):
-            ids = laneid_ref[:, pl.ds(128 * p, 128)]
-            c, s = waves_at(ids * far, count, inverse)
-            phase[j, 0, p] = c
-            phase[j, 1, p] = s
-        for p in range(6):
-            ids = rowid_ref[pl.ds(128 * p, 128), :]
-            c, s = waves_at(ids * lane, count, inverse)
-            c1 = jnp.broadcast_to(c[:, 64:65], shape)
-            s1 = jnp.broadcast_to(s[:, 64:65], shape)
-            c1, s1 = c1 * c1 - s1 * s1, 2.0 * c1 * s1
-            table[j, pl.ds(128 * p, 128), pl.ds(0, 128)] = c.astype(jnp.bfloat16)
-            table[j, pl.ds(768 + 128 * p, 128), pl.ds(0, 128)] = (-s).astype(jnp.bfloat16)
-            table[j, pl.ds(128 * p, 128), pl.ds(128, 128)] = (c * c1 - s * s1).astype(jnp.bfloat16)
-            table[j, pl.ds(768 + 128 * p, 128), pl.ds(128, 128)] = (-(s * c1 + c * s1)).astype(jnp.bfloat16)
-        return carry
-
-    lax.fori_loop(0, 16, tables, 0)
+    lax.fori_loop(8, 16, tables, 0)
 
     mine.wait()
     for d in range(1, SRC):
@@ -237,7 +271,7 @@
         return out * (640.0 ** -0.5)
 
     def copy_b(d, c):
-        to = lax.rem(h + d, DST)
+        to = tile_at(h, *TILES[d - 1])
         return pltpu.make_async_remote_copy(
             src_ref=send_b.at[c, to], dst_ref=out_ref.at[h, pl.ds(96 * c, 96), :],
             send_sem=sent_b.at[c, d], recv_sem=came_b.at[c, d], device_id=(g, to), device_id_type=MESH,
@@ -276,15 +310,13 @@
 
 
 def winds_of(spectral, legendre, tracers, wave_ids, points):
-    ids = jnp.zeros((6, 3, 40), jnp.float32).reshape(18, 40).at[:16].set(wave_ids.reshape(16, 40).astype(jnp.float32))
-    ids = jnp.pad(ids.reshape(6, 120), ((0, 0), (0, 8))).reshape(768)
-    rowid = jnp.broadcast_to(ids[:, None], (768, 128))
-    laneid = jnp.broadcast_to(ids[None, :], (8, 768))
+    ids = jnp.pad(wave_ids.reshape(16, 40), ((0, 2), (0, 0)))
+    ids = jnp.pad(ids.reshape(6, 120), ((0, 2), (0, 8)))
     vmem = pl.BlockSpec(memory_space=pltpu.VMEM)
     hbm = pl.BlockSpec(memory_space=pl.ANY)
     return pl.pallas_call(
         spectral_kernel,
-        in_specs=[hbm, hbm, hbm, vmem, vmem, pl.BlockSpec(memory_space=pltpu.SMEM)],
+        in_specs=[hbm, hbm, hbm, vmem, pl.BlockSpec(memory_space=pltpu.SMEM)],
         out_specs=[hbm] * 5,
         out_shape=[
             jax.ShapeDtypeStruct((8, 384, 256), jnp.bfloat16),
@@ -299,12 +331,17 @@
             pltpu.VMEM((3, 5, 1280, 256), jnp.bfloat16),
             pltpu.VMEM((2, 16, 8, 16, 256), jnp.bfloat16),
             pltpu.VMEM((2, 256, 128), jnp.float32),
+            pltpu.VMEM((2, 256, 128), jnp.float32),
+            pltpu.VMEM((2, 256, 128), jnp.float32),
+            pltpu.VMEM((2, 256, 128), jnp.float32),
             pltpu.VMEM((256, 128), jnp.float32),
             pltpu.VMEM((64, 16, 256), jnp.bfloat16),
             pltpu.VMEM((64, 16, 256), jnp.bfloat16),
             pltpu.VMEM((256, 128), jnp.bfloat16),
             pltpu.VMEM((64, 16, 256), jnp.bfloat16),
             pltpu.VMEM((256, 128), jnp.bfloat16),
+            pltpu.VMEM((768, 128), jnp.float32),
+            pltpu.VMEM((8, 768), jnp.float32),
             pltpu.VMEM((2, 1920, 128), jnp.float32),
             pltpu.VMEM((16, 16, 16, 128), jnp.bfloat16),
             pltpu.VMEM((16, 16, 16, 128), jnp.bfloat16),
@@ -329,7 +366,7 @@
             collective_id=0, has_side_effects=True, vmem_limit_bytes=60 * 1024 * 1024
         ),
         name="winds",
-    )(spectral, legendre, tracers, rowid, laneid, points)
+    )(spectral, legendre, tracers, ids, points)
 
 
 def rows_of(ref, start, size, stride):
@@ -337,21 +374,23 @@
 
 
 def chem_kernel(
-    ids_ref, tr_ref, wind_ref, north_ref, south_ref, east_ref, west_ref, mask_ref, base_ref, temp_ref, *rest
+    ids_ref, pts_ref, tr_ref, wind_ref, north_ref, south_ref, east_ref, west_ref, base_ref, temp_ref, *rest
 ):
     out_ref, got_ref, wide, east, west, mix, *kept = rest
     towers, moved, moved_b = kept[:2], kept[2:4], kept[4:6]
     chosen, sent, came, own = kept[6:]
     step = pl.program_id(0)
     g, tile = lax.axis_index("lat"), lax.axis_index("lon")
-    h = lax.rem(tile + 1 + step, DST)
+    h = tile_of_step(tile, step)
     levels = out_ref.shape[1]
     barrier = pltpu.get_barrier_semaphore()
 
+    place = got_ref.at[:, :, :, pl.ds(pl.multiple_of(tile * 256, 256), 256)]
+
     def send(d):
-        to = lax.rem(tile + d, DST)
+        to = tile_of_step(tile, d - 1)
         return pltpu.make_async_remote_copy(
-            src_ref=chosen.at[to], dst_ref=got_ref.at[tile], send_sem=sent.at[d], recv_sem=came.at[d],
+            src_ref=chosen.at[to], dst_ref=place, send_sem=sent.at[d], recv_sem=came.at[d],
             device_id=(g, to), device_id_type=MESH,
         )
 
@@ -379,7 +418,12 @@
     for k in range(2):
         wide[k] = wind_ref[0, :, 128 * k : 128 * k + 128].astype(jnp.float32)
     lane = lax.broadcasted_iota(jnp.int32, (16, 128), 1)
-    mask = mask_ref[...]
+    row = lax.broadcasted_iota(jnp.int32, (16, 256), 0)
+    limit = jnp.zeros((16, 256), jnp.int32)
+    for j in range(16):
+        limit = jnp.where(row == j, pts_ref[j], limit)
+    column = lax.broadcasted_iota(jnp.int32, (16, 256), 1) + tile * 256
+    mask = jnp.where(column < limit, 1.0, 0.0)
 
     def advect(l, kept, kept_b, tower):
         at = h * 8 + l
@@ -446,34 +490,33 @@
 
     @pl.when(step == DST - 1)
     def _():
-        mine = pltpu.make_async_copy(chosen.at[tile], got_ref.at[tile], own)
+        mine = pltpu.make_async_copy(chosen.at[tile], place, own)
         mine.start()
         mine.wait()
         for d in range(1, DST):
             send(d).wait()
 
 
-def chemistry(tracers, winds, north, south, east, west, mask, base, temp, ids):
-    whole = lambda s, i: (0, 0)
-    source = lambda s: lax.rem(lax.axis_index("lon") + 1 + s, DST)
+def chemistry(tracers, winds, north, south, east, west, base, temp, ids, points):
+    whole = lambda s, i, p: (0, 0)
+    source = lambda s: tile_of_step(lax.axis_index("lon"), s)
     hbm = pl.BlockSpec(memory_space=pl.ANY)
     return pl.pallas_call(
         chem_kernel,
         grid_spec=pltpu.PrefetchScalarGridSpec(
-            num_scalar_prefetch=1,
+            num_scalar_prefetch=2,
             grid=(8,),
             in_specs=[
-                pl.BlockSpec((16, 8, 16, 256), lambda s, i: (0, source(s), 0, 0)),
-                pl.BlockSpec((1, 384, 256), lambda s, i: (source(s), 0, 0)),
-                pl.BlockSpec((8, 16, 256), lambda s, i: (source(s), 0, 0)),
-                pl.BlockSpec((8, 16, 256), lambda s, i: (source(s), 0, 0)),
+                pl.BlockSpec((16, 8, 16, 256), lambda s, i, p: (0, source(s), 0, 0)),
+                pl.BlockSpec((1, 384, 256), lambda s, i, p: (source(s), 0, 0)),
+                pl.BlockSpec((8, 16, 256), lambda s, i, p: (source(s), 0, 0)),
+                pl.BlockSpec((8, 16, 256), lambda s, i, p: (source(s), 0, 0)),
                 pl.BlockSpec((256, 128), whole),
                 pl.BlockSpec((256, 128), whole),
-                pl.BlockSpec((16, 256), whole),
                 pl.BlockSpec((16, 16), whole),
                 pl.BlockSpec((16, 16), whole),
             ],
-            out_specs=[pl.BlockSpec((16, 8, 16, 256), lambda s, i: (0, source(s), 0, 0)), hbm],
+            out_specs=[pl.BlockSpec((16, 8, 16, 256), lambda s, i, p: (0, source(s), 0, 0)), hbm],
             scratch_shapes=[
                 pltpu.VMEM((2, 384, 128), jnp.float32),
                 pltpu.VMEM((256, 128), jnp.float32),
@@ -493,24 +536,21 @@
         ),
         out_shape=[
             jax.ShapeDtypeStruct((16, 64, 16, 256), jnp.bfloat16),
-            jax.ShapeDtypeStruct((8, 4, 8, 16, 256), jnp.bfloat16),
+            jax.ShapeDtypeStruct((4, 8, 16, 2048), jnp.bfloat16),
         ],
         compiler_params=pltpu.CompilerParams(collective_id=1, has_side_effects=True),
         name="chemistry",
-    )(ids, tracers, winds, north, south, east, west, mask, base, temp)
+    )(ids, points, tracers, winds, north, south, east, west, base, temp)
 
 
 def body(spectral, legendre, wave_ids, points, tracers, react_base, react_temp, active_ids):
     winds, north, south, east, west = winds_of(
         spectral.reshape(48, 40, 1280), legendre, tracers, wave_ids, points
     )
-    columns = lax.axis_index("lon") * 256 + jnp.arange(256)
-    mask = (columns[None, :] < points[:, None]).astype(jnp.float32)
     fresh, active = chemistry(
-        tracers, winds, north, south, east, west, mask, react_base, react_temp, active_ids
+        tracers, winds, north, south, east, west, react_base, react_temp, active_ids, points
     )
-    active = jnp.transpose(active, (1, 2, 3, 0, 4)).reshape(4, 8, 16, 2048).astype(jnp.float32)
-    return (fresh, active)
+    return (fresh, active.astype(jnp.float32))
 
 
 def solution(mesh):

time: 118 us -> 124 us (1.051)
  the two profiles are of different devices: /device:TPU:32 before, /device:TPU:25 now
where the time goes in v3:
time: 124 us
  Pallas kernels  110 us (89%)
  local copies, waits for them, and re-layouts  8.96 us (7%)
  other arithmetic  4.13 us (3%)
    pallas_call x1, Pallas kernels, winds_of(): pl.pallas_call(spectral_kernel, in_specs=[hbm, hbm, hbm, vmem, pl.BlockSp...  76.3 us
    pallas_call x1, Pallas kernels, chemistry(): pl.pallas_call(chem_kernel, grid_spec=pltpu.PrefetchScalarGridSpec(num_sc...  34.1 us
    unnamed x1, local copies, waits for them, and re-layouts  7.52 us
    convert_element_type x1, other arithmetic, body(): return (fresh, active.astype(jnp.float32))  4.13 us

profile of v3, /device:TPU:25, one launch (start us, length us, event | category | flops | bytes accessed | tf_op | source)
XLA Modules:
  0.0 124.2 jit_solution(15733428763032674498)
XLA Ops:
  0.6 0.8 reshape.14
  1.4 0.1 reshape.15
  1.5 0.6 pad.9.ids_ref
  2.1 76.3 %winds.1 = (bf16[8,384,256]{2,1,0:T(8,128)(2,1)}, bf16[64,16,256]{2,1,0:T(8,128)(2,1)}, bf16[64,16,256]{2,1,0:T(8,128)(2,1)}, bf16[256,128]{1,0:T(8,128)(2,1)}, bf16[256,128]{1,0:T(8,128)(2,1)}) custom-call(bf16[48,40,1280]{2,1,0:T(8,128)(2,1)} %bitcast.1, bf16[40,1280,256]{2,1,0:T(8,128)(2,1)} %leg_ref.1, bf16[16,64,16,256]{3,2,1,0:T(8,128)(2,1)} %tr_ref.3, ...), custom_call_target="tpu_custom_call" | custom-call | tf_op jit(solution)/shard_map/winds/pallas_call | solution.py:317
  78.4 34.1 %chemistry.1 = (bf16[16,64,16,256]{3,2,1,0:T(8,128)(2,1)}, bf16[4,8,16,2048]{3,2,1,0:T(8,128)(2,1)}) custom-call(s32[4]{0:T(128)} %ids_ref.1, s32[16]{0:T(128)} %pts_ref.3, bf16[16,64,16,256]{3,2,1,0:T(8,128)(2,1)} %tr_ref.3, bf16[8,384,256]{2,1,0:T(8,128)(2,1)} %get-tuple-element.9.wind_ref, bf16[64,16,256]{2,1,0:T(8,128)(2,1)} %get-tuple-element.10.north_ref, ...), custom_call_target="tpu_custom_call" | custom-call | tf_op jit(solution)/shard_map/chemistry/pallas_call | solution.py:504
  112.5 4.1 %convert_element_type.3 = f32[4,8,16,2048]{3,2,1,0:T(8,128)} convert(bf16[4,8,16,2048]{3,2,1,0:T(8,128)(2,1)} %get-tuple-element.15) | non-fusion elementwise | flops 1048576 | bytes 6291456 | tf_op jit(solution)/shard_map/convert_element_type | solution.py:553
  116.7 7.5 %copy.11 = bf16[16,64,16,256]{3,2,1,0:T(8,128)(2,1)} copy(bf16[16,64,16,256]{3,2,1,0:T(8,128)(2,1)} %get-tuple-element.18) | data formatting | bytes 16777216
  (1 shorter events, 0.0 us)

commit v4 on v3

--- a/solution.py
+++ b/solution.py
@@ -11,11 +11,13 @@
 
 
 SRC = 16
+PLANE = 136
 UNROLL = 4
 CHUNK = 8
 DST = 8
 MESH = pl.DeviceIdType.MESH
 TILES = ((2, 1), (2, 0), (1, 1), (3, 0), (3, 1), (1, 0), (0, 1))
+ORDER = ((1, 0), (3, 1), (1, 1), (3, 0), (0, 1), (2, 0), (2, 1))
 BANDS = (
     (1, 2, 0), (1, 2, 1), (0, 1, 0), (1, 0, 0), (0, 3, 1), (1, 1, 0), (0, 2, 0), (1, 3, 1),
     (0, 1, 1), (1, 0, 1), (0, 3, 0), (1, 1, 1), (0, 2, 1), (1, 3, 0), (0, 0, 1),
@@ -36,10 +38,15 @@
     return high * 8 + lax.rem(lax.rem(g // 2, 4) + dy, 4) * 2 + lax.rem(lax.rem(g, 2) + dc, 2)
 
 
-def tile_of_step(h, s):
-    power = (1 + 3 * lax.rem(s, 2)) * (1 + 15 * lax.rem(s // 2, 2)) * (1 + 255 * (s // 4))
-    code = sum(dx * 4**k for k, (dx, dz) in enumerate(TILES))
-    return lax.rem(h // 2 + lax.rem(code // power, 4), 4) * 2 + lax.rem(lax.rem(h, 2) + 1 + s, 2)
+def tile_of_step(h, step):
+    late = step // 14
+    s = lax.rem(step, 7) * (1 - late) + 7 * late
+    part = step // 7 - 2 * late + late * lax.rem(step, 2)
+    two = (1 + lax.rem(s, 2)) * (1 + 3 * lax.rem(s // 2, 2)) * (1 + 15 * (s // 4))
+    code_x = sum(dx * 4**k for k, (dx, dz) in enumerate(ORDER))
+    code_z = sum(dz * 2**k for k, (dx, dz) in enumerate(ORDER))
+    x = lax.rem(h // 2 + lax.rem(code_x // (two * two), 4), 4)
+    return x * 2 + lax.rem(lax.rem(h, 2) + lax.rem(code_z // two, 2), 2), part
 
 
 def waves_at(product, count, inverse):
@@ -90,6 +97,7 @@
         ids = jnp.broadcast_to(ids_ref[p : p + 1, :], (128, 128)).astype(jnp.float32)
         laneid[:, 128 * p : 128 * p + 128] = ids[:8]
         rowid[128 * p : 128 * p + 128, :] = ids.T
+    tall[...] = jnp.zeros_like(tall)
     empty[...] = jnp.zeros_like(empty)
     blank_cols[...] = jnp.zeros_like(blank_cols)
     cols[...] = jnp.zeros_like(cols)
@@ -138,12 +146,17 @@
             rows = [spread[k, pl.ds(m, 48, stride=40), :].astype(jnp.bfloat16) for k in range(10)]
             value = jnp.dot(jnp.concatenate(rows, axis=1), leg[slot, w], preferred_element_type=jnp.float32)
             for k in range(2):
-                tall[k, pl.ds(48 * m, 48), :] = value[:, 128 * k : 128 * k + 128]
+                for q in range(6):
+                    part = value[8 * q : 8 * q + 8, 128 * k : 128 * k + 128]
+                    tall[k, pl.ds(20 * q + lax.rem(m, 20), 8, stride=PLANE), :] = part
 
         @pl.when(i < 5)
         def _():
             leg_copy(i + 3).start()
 
+        return carry
+
+    def edges(i, carry):
         side = lax.rem(i, 2)
         band_copy(i).wait()
 
@@ -170,32 +183,9 @@
 
         return carry
 
-    lax.fori_loop(0, 8, step, 0)
+    lax.fori_loop(0, 8, edges, 0)
     edge[...] = cols[...].astype(jnp.bfloat16)
-    blank = jnp.zeros((8, 128), jnp.float32)
-
-    def turn(r, carry):
-        for k in range(2):
-            parts = [tall[k, pl.ds(16 * f + r, 40, stride=48), :] for f in range(3)]
-            block = jnp.concatenate(parts + [blank], axis=0).T.astype(jnp.bfloat16)
-            for b in range(8):
-                send_a[8 * k + b, r] = block[16 * b : 16 * b + 16]
-        return carry
-
-    lax.fori_loop(0, 16, turn, 0)
     pl.semaphore_wait(barrier, SRC + DST - 2)
-
-    def copy_a(d):
-        to = band_at(g, *BANDS[d - 1])
-        return pltpu.make_async_remote_copy(
-            src_ref=send_a.at[to], dst_ref=got_a.at[g], send_sem=sent_a.at[d], recv_sem=came_a.at[d],
-            device_id=(to, h), device_id_type=MESH,
-        )
-
-    for d in range(1, SRC):
-        copy_a(d).start()
-    mine = pltpu.make_async_copy(send_a.at[g], got_a.at[g], own.at[0])
-    mine.start()
 
     def halo(k, src, dst, lat, lon):
         return pltpu.make_async_remote_copy(
@@ -221,38 +211,62 @@
         pl.when(sends)(copy.start)
         pl.when(jnp.logical_not(gets))(fill.start)
 
-    lax.fori_loop(8, 16, tables, 0)
-
+    def turn(half):
+        def pair(i, carry):
+            for k in range(2):
+                blocks = [tall[k, pl.ds(PLANE * (2 * i + n), 128), :].T for n in range(2)]
+                for b in range(8):
+                    for rows in range(2):
+                        at = 16 * b + 8 * rows
+                        both = jnp.concatenate([block[at : at + 8] for block in blocks], axis=0)
+                        send_a[8 * k + b, half, rows, pl.ds(16 * i, 16), :] = both.astype(jnp.bfloat16)
+            return carry
+
+        lax.fori_loop(0, 4, pair, 0)
+
+    def copy_a(d, k):
+        to = band_at(g, *BANDS[d - 1])
+        src, dst = ((send_a.at[to, 0], got_a.at[g, 0]), (send_a.at[to, 1, 0], got_a.at[g, 1, 0]),
+                    (send_a.at[to, 1, 1], got_a.at[g, 1, 1]))[k]
+        return pltpu.make_async_remote_copy(
+            src_ref=src, dst_ref=dst, send_sem=sent_a.at[k, d], recv_sem=came_a.at[k, d],
+            device_id=(to, h), device_id_type=MESH,
+        )
+
+    lax.fori_loop(0, 4, step, 0)
+    turn(0)
+    for d in range(1, SRC):
+        copy_a(d, 0).start()
+    lax.fori_loop(4, 8, step, 0)
+    turn(1)
+    for k in (1, 2):
+        for d in range(1, SRC):
+            copy_a(d, k).start()
+    mine = pltpu.make_async_copy(send_a.at[g], got_a.at[g], own.at[0])
+    mine.start()
+    lax.fori_loop(8, 12, tables, 0)
     mine.wait()
-    for d in range(1, SRC):
-        copy_a(d).wait_recv()
-
-    def widen(q, carry):
-        coef[pl.ds(256 * q, 256), :] = got_a[q].reshape(256, 128).astype(jnp.float32)
-        return carry
-
-    lax.fori_loop(0, SRC, widen, 0)
+
+    def widen(rows):
+        def one(q, carry):
+            for half in range(2):
+                coef[pl.ds(64 * (2 * q + half), 64), :] = got_a[q, half, rows].astype(jnp.float32)
+            return carry
+
+        lax.fori_loop(0, SRC, one, 0)
 
     def turn_of(j):
-        lane = lax.broadcasted_iota(jnp.int32, (16, 128), 1)
+        lane = lax.broadcasted_iota(jnp.int32, (8, 128), 1)
+        row = lax.rem(j, 8)
         for p in range(6):
-            held = []
-            for q in range(3):
-                s = 3 * p + q
-                if s < SRC:
-                    held.append(coef[pl.ds(256 * s + j, 16, stride=16), :])
-                else:
-                    held.append(None)
-            for f in range(3):
-                value = jnp.zeros((16, 128), jnp.float32)
-                for q in range(3):
-                    if held[q] is None:
-                        continue
-                    moved = held[q] if q == f else pltpu.roll(held[q], (40 * (q - f)) % 128, 1)
-                    value = jnp.where((lane >= 40 * q) & (lane < 40 * q + 40), moved, value)
-                re, im = value[:8], value[8:]
-                line[f, 0, p] = re
-                line[f, 1, p] = im
+            count = min(6, 2 * SRC - 6 * p)
+            held = [coef[pl.ds(64 * (6 * p + q) + row, 8, stride=8), :] for q in range(count)]
+            for f in range(6):
+                value = jnp.zeros((8, 128), jnp.float32)
+                for q in range(count):
+                    moved = held[q] if q == f else pltpu.roll(held[q], (20 * (q - f)) % 128, 1)
+                    value = jnp.where((lane >= 20 * q) & (lane < 20 * q + 20), moved, value)
+                line[f // 2, f % 2, p] = value
         for p in range(6):
             for a in range(0, DST, 2):
                 parts = []
@@ -292,9 +306,17 @@
         copy_own(c).start()
         return carry
 
-    lax.fori_loop(0, 4, quad, 0)
-    for d in range(1, SRC):
-        copy_a(d).wait_send()
+    for rows in range(2):
+        for k in ((0, 1), (2,))[rows]:
+            for d in range(1, SRC):
+                copy_a(d, k).wait_recv()
+        widen(rows)
+        lax.fori_loop(2 * rows, 2 * rows + 2, quad, 0)
+        if rows == 0:
+            lax.fori_loop(12, 16, tables, 0)
+    for k in range(3):
+        for d in range(1, SRC):
+            copy_a(d, k).wait_send()
 
     def finish(c, carry):
         copy_own(c).wait()
@@ -310,7 +332,7 @@
 
 
 def winds_of(spectral, legendre, tracers, wave_ids, points):
-    ids = jnp.pad(wave_ids.reshape(16, 40), ((0, 2), (0, 0)))
+    ids = jnp.pad(wave_ids.reshape(32, 20), ((0, 4), (0, 0)))
     ids = jnp.pad(ids.reshape(6, 120), ((0, 2), (0, 8)))
     vmem = pl.BlockSpec(memory_space=pltpu.VMEM)
     hbm = pl.BlockSpec(memory_space=pl.ANY)
@@ -342,17 +364,17 @@
             pltpu.VMEM((256, 128), jnp.bfloat16),
             pltpu.VMEM((768, 128), jnp.float32),
             pltpu.VMEM((8, 768), jnp.float32),
-            pltpu.VMEM((2, 1920, 128), jnp.float32),
-            pltpu.VMEM((16, 16, 16, 128), jnp.bfloat16),
-            pltpu.VMEM((16, 16, 16, 128), jnp.bfloat16),
+            pltpu.VMEM((2, 8 * PLANE, 128), jnp.float32),
+            pltpu.VMEM((16, 2, 2, 64, 128), jnp.bfloat16),
+            pltpu.VMEM((16, 2, 2, 64, 128), jnp.bfloat16),
             pltpu.VMEM((16, 1536, 256), jnp.bfloat16),
             pltpu.VMEM((16, 2, 6, 8, 128), jnp.float32),
-            pltpu.VMEM((4096, 128), jnp.float32),
+            pltpu.VMEM((2048, 128), jnp.float32),
             pltpu.VMEM((3, 2, 6, 8, 128), jnp.float32),
             pltpu.VMEM((192, 1536), jnp.bfloat16),
             pltpu.VMEM((4, 8, 96, 256), jnp.bfloat16),
-            pltpu.SemaphoreType.DMA((16,)),
-            pltpu.SemaphoreType.DMA((16,)),
+            pltpu.SemaphoreType.DMA((3, 16)),
+            pltpu.SemaphoreType.DMA((3, 16)),
             pltpu.SemaphoreType.DMA((4, 8)),
             pltpu.SemaphoreType.DMA((4, 8)),
             pltpu.SemaphoreType.DMA((9,)),
@@ -381,16 +403,17 @@
     chosen, sent, came, own = kept[6:]
     step = pl.program_id(0)
     g, tile = lax.axis_index("lat"), lax.axis_index("lon")
-    h = tile_of_step(tile, step)
+    h, part = tile_of_step(tile, step)
     levels = out_ref.shape[1]
     barrier = pltpu.get_barrier_semaphore()
 
     place = got_ref.at[:, :, :, pl.ds(pl.multiple_of(tile * 256, 256), 256)]
 
     def send(d):
-        to = tile_of_step(tile, d - 1)
+        to, some = tile_of_step(tile, d)
+        rows = pl.ds(4 * some, 4)
         return pltpu.make_async_remote_copy(
-            src_ref=chosen.at[to], dst_ref=place, send_sem=sent.at[d], recv_sem=came.at[d],
+            src_ref=chosen.at[to, :, rows], dst_ref=place.at[:, rows], send_sem=sent.at[d], recv_sem=came.at[d],
             device_id=(g, to), device_id_type=MESH,
         )
 
@@ -426,8 +449,8 @@
     mask = jnp.where(column < limit, 1.0, 0.0)
 
     def advect(l, kept, kept_b, tower):
-        at = h * 8 + l
-        local = l
+        at = h * 8 + 4 * part + l
+        local = 4 * part + l
         u = 0.1 * rows_of(wide, local, 16, 24)
         v = 0.1 * rows_of(wide, 8 + local, 16, 24)
         east_w, west_w = (0.05 - u) * mask, (0.05 + u) * mask
@@ -455,7 +478,7 @@
             kept_b[pl.ds(16 * t, 16), :] = q.astype(jnp.bfloat16)
 
     def settle(l, kept, kept_b):
-        temper = rows_of(wide, 16 + l, 16, 24)
+        temper = rows_of(wide, 16 + 4 * part + l, 16, 24)
         for c in range(0, 16, CHUNK):
             y = jnp.dot(mix[pl.ds(32 * c, 32 * CHUNK), :], kept_b[...], preferred_element_type=jnp.float32)
             for t in range(CHUNK):
@@ -464,7 +487,7 @@
                 kept[c + t] = q
                 out_ref[c + t, l] = q.astype(jnp.bfloat16)
         for a in range(4):
-            chosen[h, a, l] = kept[ids_ref[a]].astype(jnp.bfloat16)
+            chosen[h, a, 4 * part + l] = kept[ids_ref[a]].astype(jnp.bfloat16)
 
     def several(i, carry):
         pend = None
@@ -484,39 +507,49 @@
     def _():
         pl.semaphore_wait(barrier, DST - 1)
 
-    @pl.when(step < DST - 1)
+    @pl.when(step < 14)
     def _():
-        send(step + 1).start()
-
-    @pl.when(step == DST - 1)
+        send(step).start()
+
+    @pl.when(step == 15)
     def _():
         mine = pltpu.make_async_copy(chosen.at[tile], place, own)
         mine.start()
         mine.wait()
-        for d in range(1, DST):
+        for d in range(14):
             send(d).wait()
 
 
 def chemistry(tracers, winds, north, south, east, west, base, temp, ids, points):
     whole = lambda s, i, p: (0, 0)
-    source = lambda s: tile_of_step(lax.axis_index("lon"), s)
     hbm = pl.BlockSpec(memory_space=pl.ANY)
+
+    def rows(s, i, p):
+        tile, part = tile_of_step(lax.axis_index("lon"), s)
+        return (2 * tile + part, 0, 0)
+
+    def cube(s, i, p):
+        return (0,) + rows(s, i, p)
+
+    def source(s, i, p):
+        return (tile_of_step(lax.axis_index("lon"), s)[0], 0, 0)
+
     return pl.pallas_call(
         chem_kernel,
         grid_spec=pltpu.PrefetchScalarGridSpec(
             num_scalar_prefetch=2,
-            grid=(8,),
+            grid=(16,),
             in_specs=[
-                pl.BlockSpec((16, 8, 16, 256), lambda s, i, p: (0, source(s), 0, 0)),
-                pl.BlockSpec((1, 384, 256), lambda s, i, p: (source(s), 0, 0)),
-                pl.BlockSpec((8, 16, 256), lambda s, i, p: (source(s), 0, 0)),
-                pl.BlockSpec((8, 16, 256), lambda s, i, p: (source(s), 0, 0)),
+                pl.BlockSpec((16, 4, 16, 256), cube),
+                pl.BlockSpec((1, 384, 256), source),
+                pl.BlockSpec((4, 16, 256), rows),
+                pl.BlockSpec((4, 16, 256), rows),
                 pl.BlockSpec((256, 128), whole),
                 pl.BlockSpec((256, 128), whole),
                 pl.BlockSpec((16, 16), whole),
                 pl.BlockSpec((16, 16), whole),
             ],
-            out_specs=[pl.BlockSpec((16, 8, 16, 256), lambda s, i, p: (0, source(s), 0, 0)), hbm],
+            out_specs=[pl.BlockSpec((16, 4, 16, 256), cube), hbm],
             scratch_shapes=[
                 pltpu.VMEM((2, 384, 128), jnp.float32),
                 pltpu.VMEM((256, 128), jnp.float32),
@@ -529,8 +562,8 @@
                 pltpu.VMEM((256, 256), jnp.bfloat16),
                 pltpu.VMEM((256, 256), jnp.bfloat16),
                 pltpu.VMEM((8, 4, 8, 16, 256), jnp.bfloat16),
-                pltpu.SemaphoreType.DMA((8,)),
-                pltpu.SemaphoreType.DMA((8,)),
+                pltpu.SemaphoreType.DMA((14,)),
+                pltpu.SemaphoreType.DMA((14,)),
                 pltpu.SemaphoreType.DMA,
             ],
         ),

time: 124 us -> 108 us (0.87)
  Pallas kernels: 110 us -> 94.1 us
    pallas_call x1, Pallas kernels: 76.3 us -> 60.5 us  [winds_of(): pl.pallas_call(spectral_kernel, in_specs=[hbm, hbm, hbm, vmem, pl.BlockSp...]
where the time goes in v4:
time: 108 us
  Pallas kernels  94.1 us (87%)
  local copies, waits for them, and re-layouts  8.98 us (8%)
  other arithmetic  4.13 us (4%)
    pallas_call x1, Pallas kernels, winds_of(): pl.pallas_call(spectral_kernel, in_specs=[hbm, hbm, hbm, vmem, pl.BlockSp...  60.5 us
    pallas_call x1, Pallas kernels, chemistry(): pl.pallas_call(chem_kernel, grid_spec=pltpu.PrefetchScalarGridSpec(num_sc...  33.6 us
    unnamed x1, local copies, waits for them, and re-layouts  7.52 us
    convert_element_type x1, other arithmetic, body(): return (fresh, active.astype(jnp.float32))  4.13 us

profile of v4, /device:TPU:25, one launch (start us, length us, event | category | flops | bytes accessed | tf_op | source)
XLA Modules:
  0.0 107.8 jit_solution(14140762951232219267)
XLA Ops:
  0.6 0.8 reshape.14
  1.4 0.1 reshape.15
  1.5 0.6 pad.9.ids_ref
  2.1 60.5 %winds.1 = (bf16[8,384,256]{2,1,0:T(8,128)(2,1)}, bf16[64,16,256]{2,1,0:T(8,128)(2,1)}, bf16[64,16,256]{2,1,0:T(8,128)(2,1)}, bf16[256,128]{1,0:T(8,128)(2,1)}, bf16[256,128]{1,0:T(8,128)(2,1)}) custom-call(bf16[48,40,1280]{2,1,0:T(8,128)(2,1)} %bitcast.1, bf16[40,1280,256]{2,1,0:T(8,128)(2,1)} %leg_ref.1, bf16[16,64,16,256]{3,2,1,0:T(8,128)(2,1)} %tr_ref.3, ...), custom_call_target="tpu_custom_call" | custom-call | tf_op jit(solution)/shard_map/winds/pallas_call | solution.py:339
  62.6 33.6 %chemistry.1 = (bf16[16,64,16,256]{3,2,1,0:T(8,128)(2,1)}, bf16[4,8,16,2048]{3,2,1,0:T(8,128)(2,1)}) custom-call(s32[4]{0:T(128)} %ids_ref.1, s32[16]{0:T(128)} %pts_ref.3, bf16[16,64,16,256]{3,2,1,0:T(8,128)(2,1)} %tr_ref.3, bf16[8,384,256]{2,1,0:T(8,128)(2,1)} %get-tuple-element.9.wind_ref, bf16[64,16,256]{2,1,0:T(8,128)(2,1)} %get-tuple-element.10.north_ref, ...), custom_call_target="tpu_custom_call" | custom-call | tf_op jit(solution)/shard_map/chemistry/pallas_call | solution.py:537
  96.2 4.1 %convert_element_type.3 = f32[4,8,16,2048]{3,2,1,0:T(8,128)} convert(bf16[4,8,16,2048]{3,2,1,0:T(8,128)(2,1)} %get-tuple-element.15) | non-fusion elementwise | flops 1048576 | bytes 6291456 | tf_op jit(solution)/shard_map/convert_element_type | solution.py:586
  100.3 7.5 %copy.11 = bf16[16,64,16,256]{3,2,1,0:T(8,128)(2,1)} copy(bf16[16,64,16,256]{3,2,1,0:T(8,128)(2,1)} %get-tuple-element.18) | data formatting | bytes 16777216
  (1 shorter events, 0.0 us)

commit v5 on v4

--- a/solution.py
+++ b/solution.py
@@ -17,7 +17,7 @@
 DST = 8
 MESH = pl.DeviceIdType.MESH
 TILES = ((2, 1), (2, 0), (1, 1), (3, 0), (3, 1), (1, 0), (0, 1))
-ORDER = ((1, 0), (3, 1), (1, 1), (3, 0), (0, 1), (2, 0), (2, 1))
+ORDER = ((2, 0), (0, 1), (2, 1), (1, 0), (3, 1), (1, 1), (3, 0))
 BANDS = (
     (1, 2, 0), (1, 2, 1), (0, 1, 0), (1, 0, 0), (0, 3, 1), (1, 1, 0), (0, 2, 0), (1, 3, 1),
     (0, 1, 1), (1, 0, 1), (0, 3, 0), (1, 1, 1), (0, 2, 1), (1, 3, 0), (0, 0, 1),
@@ -79,7 +79,7 @@
     wide = (wide_0, wide_1, wide_2, wide_3)
 
     def leg_copy(i):
-        slot = lax.rem(i, 3)
+        slot = lax.rem(i, 5)
         return pltpu.make_async_copy(leg_ref.at[pl.ds(5 * i, 5)], leg.at[slot], leg_in.at[slot])
 
     def band_copy(i):
@@ -87,30 +87,24 @@
         return pltpu.make_async_copy(tr_ref.at[:, pl.ds(8 * i, 8)], band.at[slot], band_in.at[slot])
 
     spec_copy = pltpu.make_async_copy(spec_ref, spec, taken)
+    band_copy(0).start()
     spec_copy.start()
-    leg_copy(0).start()
-    band_copy(0).start()
-    leg_copy(1).start()
     band_copy(1).start()
-    leg_copy(2).start()
+    place = lax.broadcasted_iota(jnp.int32, (8, 128), 1)
     for p in range(6):
-        ids = jnp.broadcast_to(ids_ref[p : p + 1, :], (128, 128)).astype(jnp.float32)
-        laneid[:, 128 * p : 128 * p + 128] = ids[:8]
-        rowid[128 * p : 128 * p + 128, :] = ids.T
+        at, by = divmod(120 * p, 128)
+        ids = jnp.broadcast_to(ids_ref[at : at + 1, :], (8, 128)).astype(jnp.float32)
+        if by:
+            ids = pltpu.roll(ids, 128 - by, 1)
+        if 0 < by and at < 4:
+            more = jnp.broadcast_to(ids_ref[at + 1 : at + 2, :], (8, 128)).astype(jnp.float32)
+            ids = jnp.where(place < 128 - by, ids, pltpu.roll(more, 128 - by, 1))
+        laneid[:, 128 * p : 128 * p + 128] = ids
+        rowid[128 * p : 128 * p + 128, :] = jnp.broadcast_to(ids[:1], (128, 128)).T
     tall[...] = jnp.zeros_like(tall)
     empty[...] = jnp.zeros_like(empty)
     blank_cols[...] = jnp.zeros_like(blank_cols)
     cols[...] = jnp.zeros_like(cols)
-    spec_copy.wait()
-
-    def loosen(i, carry):
-        for r in range(4):
-            for k in range(10):
-                part = spec[4 * i + r, :, 128 * k : 128 * k + 128]
-                spread[k, pl.ds(160 * i + 40 * r, 40), :] = part.astype(jnp.float32)
-        return carry
-
-    lax.fori_loop(0, 12, loosen, 0)
     lane = lax.broadcasted_iota(jnp.int32, (256, 128), 1)
 
     shape = (128, 128)
@@ -138,7 +132,7 @@
         return carry
 
     def step(i, carry):
-        slot = lax.rem(i, 3)
+        slot = lax.rem(i, 5)
         leg_copy(i).wait()
         tables(i, 0)
         for w in range(5):
@@ -150,13 +144,17 @@
                     part = value[8 * q : 8 * q + 8, 128 * k : 128 * k + 128]
                     tall[k, pl.ds(20 * q + lax.rem(m, 20), 8, stride=PLANE), :] = part
 
-        @pl.when(i < 5)
+        @pl.when(i < 3)
         def _():
-            leg_copy(i + 3).start()
+            leg_copy(i + 5).start()
 
         return carry
 
     def edges(i, carry):
+        @pl.when(i >= 3)
+        def _():
+            leg_copy(i - 3).start()
+
         side = lax.rem(i, 2)
         band_copy(i).wait()
 
@@ -233,6 +231,16 @@
             device_id=(to, h), device_id_type=MESH,
         )
 
+    spec_copy.wait()
+
+    def loosen(i, carry):
+        for r in range(4):
+            for k in range(10):
+                part = spec[4 * i + r, :, 128 * k : 128 * k + 128]
+                spread[k, pl.ds(160 * i + 40 * r, 40), :] = part.astype(jnp.float32)
+        return carry
+
+    lax.fori_loop(0, 12, loosen, 0)
     lax.fori_loop(0, 4, step, 0)
     turn(0)
     for d in range(1, SRC):
@@ -332,8 +340,6 @@
 
 
 def winds_of(spectral, legendre, tracers, wave_ids, points):
-    ids = jnp.pad(wave_ids.reshape(32, 20), ((0, 4), (0, 0)))
-    ids = jnp.pad(ids.reshape(6, 120), ((0, 2), (0, 8)))
     vmem = pl.BlockSpec(memory_space=pltpu.VMEM)
     hbm = pl.BlockSpec(memory_space=pl.ANY)
     return pl.pallas_call(
@@ -350,7 +356,7 @@
         scratch_shapes=[
             pltpu.VMEM((48, 40, 1280), jnp.bfloat16),
             pltpu.VMEM((10, 1920, 128), jnp.float32),
-            pltpu.VMEM((3, 5, 1280, 256), jnp.bfloat16),
+            pltpu.VMEM((5, 5, 1280, 256), jnp.bfloat16),
             pltpu.VMEM((2, 16, 8, 16, 256), jnp.bfloat16),
             pltpu.VMEM((2, 256, 128), jnp.float32),
             pltpu.VMEM((2, 256, 128), jnp.float32),
@@ -381,14 +387,14 @@
             pltpu.SemaphoreType.DMA((4,)),
             pltpu.SemaphoreType.DMA((4,)),
             pltpu.SemaphoreType.DMA,
-            pltpu.SemaphoreType.DMA((3,)),
+            pltpu.SemaphoreType.DMA((5,)),
             pltpu.SemaphoreType.DMA((2,)),
         ],
         compiler_params=pltpu.CompilerParams(
             collective_id=0, has_side_effects=True, vmem_limit_bytes=60 * 1024 * 1024
         ),
         name="winds",
-    )(spectral, legendre, tracers, ids, points)
+    )(spectral, legendre, tracers, wave_ids.reshape(5, 128), points)
 
 
 def rows_of(ref, start, size, stride):

time: 108 us -> 103 us (0.954)
  Pallas kernels: 94.1 us -> 90.4 us
  local copies, waits for them, and re-layouts: 8.98 us -> 7.52 us
    pallas_call x1, Pallas kernels: 60.5 us -> 58.5 us  [winds_of(): pl.pallas_call(spectral_kernel, in_specs=[hbm, hbm, hbm, vmem, pl.BlockSp...]
    pallas_call x1, Pallas kernels: 33.6 us -> 31.9 us  [chemistry(): pl.pallas_call(chem_kernel, grid_spec=pltpu.PrefetchScalarGridSpec(num_sc...]
where the time goes in v5:
time: 103 us
  Pallas kernels  90.4 us (88%)
  local copies, waits for them, and re-layouts  7.52 us (7%)
  other arithmetic  4.13 us (4%)
    pallas_call x1, Pallas kernels, winds_of(): pl.pallas_call(spectral_kernel, in_specs=[hbm, hbm, hbm, vmem, pl.BlockSp...  58.5 us
    pallas_call x1, Pallas kernels, chemistry(): pl.pallas_call(chem_kernel, grid_spec=pltpu.PrefetchScalarGridSpec(num_sc...  31.9 us
    unnamed x1, local copies, waits for them, and re-layouts  7.52 us
    convert_element_type x1, other arithmetic, body(): return (fresh, active.astype(jnp.float32))  4.13 us

profile of v5, /device:TPU:25, one launch (start us, length us, event | category | flops | bytes accessed | tf_op | source)
XLA Modules:
  0.0 102.7 jit_solution(5489076805271135029)
XLA Ops:
  0.6 58.5 %winds.1 = (bf16[8,384,256]{2,1,0:T(8,128)(2,1)}, bf16[64,16,256]{2,1,0:T(8,128)(2,1)}, bf16[64,16,256]{2,1,0:T(8,128)(2,1)}, bf16[256,128]{1,0:T(8,128)(2,1)}, bf16[256,128]{1,0:T(8,128)(2,1)}) custom-call(bf16[48,40,1280]{2,1,0:T(8,128)(2,1)} %bitcast.2, bf16[40,1280,256]{2,1,0:T(8,128)(2,1)} %leg_ref.1, bf16[16,64,16,256]{3,2,1,0:T(8,128)(2,1)} %tr_ref.3, ...), custom_call_target="tpu_custom_call" | custom-call | tf_op jit(solution)/shard_map/winds/pallas_call | solution.py:345
  59.1 31.9 %chemistry.1 = (bf16[16,64,16,256]{3,2,1,0:T(8,128)(2,1)}, bf16[4,8,16,2048]{3,2,1,0:T(8,128)(2,1)}) custom-call(s32[4]{0:T(128)} %ids_ref.1, s32[16]{0:T(128)} %pts_ref.3, bf16[16,64,16,256]{3,2,1,0:T(8,128)(2,1)} %tr_ref.3, bf16[8,384,256]{2,1,0:T(8,128)(2,1)} %get-tuple-element.9.wind_ref, bf16[64,16,256]{2,1,0:T(8,128)(2,1)} %get-tuple-element.10.north_ref, ...), custom_call_target="tpu_custom_call" | custom-call | tf_op jit(solution)/shard_map/chemistry/pallas_call | solution.py:543
  91.0 4.1 %convert_element_type.3 = f32[4,8,16,2048]{3,2,1,0:T(8,128)} convert(bf16[4,8,16,2048]{3,2,1,0:T(8,128)(2,1)} %get-tuple-element.15) | non-fusion elementwise | flops 1048576 | bytes 6291456 | tf_op jit(solution)/shard_map/convert_element_type | solution.py:592
  95.1 7.5 %copy.11 = bf16[16,64,16,256]{3,2,1,0:T(8,128)(2,1)} copy(bf16[16,64,16,256]{3,2,1,0:T(8,128)(2,1)} %get-tuple-element.18) | data formatting | bytes 16777216

commit v6 on v5

--- a/solution.py
+++ b/solution.py
@@ -17,7 +17,7 @@
 DST = 8
 MESH = pl.DeviceIdType.MESH
 TILES = ((2, 1), (2, 0), (1, 1), (3, 0), (3, 1), (1, 0), (0, 1))
-ORDER = ((2, 0), (0, 1), (2, 1), (1, 0), (3, 1), (1, 1), (3, 0))
+ORDER = ((2, 1), (0, 1), (2, 0), (1, 1), (3, 1), (1, 0), (3, 0))
 BANDS = (
     (1, 2, 0), (1, 2, 1), (0, 1, 0), (1, 0, 0), (0, 3, 1), (1, 1, 0), (0, 2, 0), (1, 3, 1),
     (0, 1, 1), (1, 0, 1), (0, 3, 0), (1, 1, 1), (0, 2, 1), (1, 3, 0), (0, 0, 1),
@@ -38,15 +38,12 @@
     return high * 8 + lax.rem(lax.rem(g // 2, 4) + dy, 4) * 2 + lax.rem(lax.rem(g, 2) + dc, 2)
 
 
-def tile_of_step(h, step):
-    late = step // 14
-    s = lax.rem(step, 7) * (1 - late) + 7 * late
-    part = step // 7 - 2 * late + late * lax.rem(step, 2)
+def tile_of_step(h, s):
     two = (1 + lax.rem(s, 2)) * (1 + 3 * lax.rem(s // 2, 2)) * (1 + 15 * (s // 4))
     code_x = sum(dx * 4**k for k, (dx, dz) in enumerate(ORDER))
     code_z = sum(dz * 2**k for k, (dx, dz) in enumerate(ORDER))
     x = lax.rem(h // 2 + lax.rem(code_x // (two * two), 4), 4)
-    return x * 2 + lax.rem(lax.rem(h, 2) + lax.rem(code_z // two, 2), 2), part
+    return x * 2 + lax.rem(lax.rem(h, 2) + lax.rem(code_z // two, 2), 2)
 
 
 def waves_at(product, count, inverse):
@@ -155,6 +152,11 @@
         def _():
             leg_copy(i - 3).start()
 
+        for n in range(3):
+            @pl.when(i == 2 * n + 3)
+            def _():
+                send_rows(n)
+
         side = lax.rem(i, 2)
         band_copy(i).wait()
 
@@ -181,33 +183,45 @@
 
         return carry
 
-    lax.fori_loop(0, 8, edges, 0)
-    edge[...] = cols[...].astype(jnp.bfloat16)
-    pl.semaphore_wait(barrier, SRC + DST - 2)
-
     def halo(k, src, dst, lat, lon):
         return pltpu.make_async_remote_copy(
             src_ref=src, dst_ref=dst, send_sem=sent_h.at[k], recv_sem=came_h.at[k],
             device_id=(lat, lon), device_id_type=MESH,
         )
 
-    to_north = halo(0, high, south_ref, lax.rem(g + 1, SRC), h)
-    to_south = halo(1, low, north_ref, lax.rem(g + SRC - 1, SRC), h)
-    to_east = halo(2, edge, west_ref, g, lax.rem(h + 1, DST))
-    to_west = halo(3, edge, east_ref, g, lax.rem(h + DST - 1, DST))
+    to_east = halo(0, edge, west_ref, g, lax.rem(h + 1, DST))
+    to_west = halo(1, edge, east_ref, g, lax.rem(h + DST - 1, DST))
+
+    def to_north(n):
+        rows = pl.ds(16 * n, 16)
+        return halo(2 + n, high.at[rows], south_ref.at[rows], lax.rem(g + 1, SRC), h)
+
+    def to_south(n):
+        rows = pl.ds(16 * n, 16)
+        return halo(6 + n, low.at[rows], north_ref.at[rows], lax.rem(g + SRC - 1, SRC), h)
+
+    def send_rows(n):
+        @pl.when(g < SRC - 1)
+        def _():
+            to_north(n).start()
+
+        @pl.when(g > 0)
+        def _():
+            to_south(n).start()
+
     none_south = pltpu.make_async_copy(empty, south_ref, own.at[5])
     none_north = pltpu.make_async_copy(empty, north_ref, own.at[6])
     none_west = pltpu.make_async_copy(blank_cols, west_ref, own.at[7])
     none_east = pltpu.make_async_copy(blank_cols, east_ref, own.at[8])
-    sides = (
-        (g < SRC - 1, to_north, g > 0, none_south),
-        (g > 0, to_south, g < SRC - 1, none_north),
-        (h < DST - 1, to_east, h > 0, none_west),
-        (h > 0, to_west, h < DST - 1, none_east),
-    )
-    for sends, copy, gets, fill in sides:
-        pl.when(sends)(copy.start)
-        pl.when(jnp.logical_not(gets))(fill.start)
+    fills = ((g == 0, none_south), (g == SRC - 1, none_north), (h == 0, none_west), (h == DST - 1, none_east))
+    pl.semaphore_wait(barrier, SRC + DST - 2)
+    lax.fori_loop(0, 8, edges, 0)
+    edge[...] = cols[...].astype(jnp.bfloat16)
+    send_rows(3)
+    pl.when(h < DST - 1)(to_east.start)
+    pl.when(h > 0)(to_west.start)
+    for here, fill in fills:
+        pl.when(here)(fill.start)
 
     def turn(half):
         def pair(i, carry):
@@ -333,10 +347,17 @@
         return carry
 
     lax.fori_loop(0, 4, finish, 0)
-    for sends, copy, gets, fill in sides:
-        pl.when(sends)(copy.wait_send)
-        pl.when(gets)(copy.wait_recv)
-        pl.when(jnp.logical_not(gets))(fill.wait)
+    pl.when(h < DST - 1)(to_east.wait_send)
+    pl.when(h > 0)(to_west.wait_send)
+    pl.when(h > 0)(to_east.wait_recv)
+    pl.when(h < DST - 1)(to_west.wait_recv)
+    for n in range(4):
+        pl.when(g < SRC - 1)(to_north(n).wait_send)
+        pl.when(g > 0)(to_south(n).wait_send)
+        pl.when(g > 0)(to_north(n).wait_recv)
+        pl.when(g < SRC - 1)(to_south(n).wait_recv)
+    for here, fill in fills:
+        pl.when(here)(fill.wait)
 
 
 def winds_of(spectral, legendre, tracers, wave_ids, points):
@@ -384,8 +405,8 @@
             pltpu.SemaphoreType.DMA((4, 8)),
             pltpu.SemaphoreType.DMA((4, 8)),
             pltpu.SemaphoreType.DMA((9,)),
-            pltpu.SemaphoreType.DMA((4,)),
-            pltpu.SemaphoreType.DMA((4,)),
+            pltpu.SemaphoreType.DMA((10,)),
+            pltpu.SemaphoreType.DMA((10,)),
             pltpu.SemaphoreType.DMA,
             pltpu.SemaphoreType.DMA((5,)),
             pltpu.SemaphoreType.DMA((2,)),
@@ -409,17 +430,18 @@
     chosen, sent, came, own = kept[6:]
     step = pl.program_id(0)
     g, tile = lax.axis_index("lat"), lax.axis_index("lon")
-    h, part = tile_of_step(tile, step)
+    h = tile_of_step(tile, step)
     levels = out_ref.shape[1]
     barrier = pltpu.get_barrier_semaphore()
 
     place = got_ref.at[:, :, :, pl.ds(pl.multiple_of(tile * 256, 256), 256)]
 
-    def send(d):
-        to, some = tile_of_step(tile, d)
-        rows = pl.ds(4 * some, 4)
+    def send(d, half):
+        to = tile_of_step(tile, d)
+        rows = pl.ds(4 * half, 4)
         return pltpu.make_async_remote_copy(
-            src_ref=chosen.at[to, :, rows], dst_ref=place.at[:, rows], send_sem=sent.at[d], recv_sem=came.at[d],
+            src_ref=chosen.at[to, :, rows], dst_ref=place.at[:, rows],
+            send_sem=sent.at[d, half], recv_sem=came.at[d, half],
             device_id=(g, to), device_id_type=MESH,
         )
 
@@ -455,8 +477,8 @@
     mask = jnp.where(column < limit, 1.0, 0.0)
 
     def advect(l, kept, kept_b, tower):
-        at = h * 8 + 4 * part + l
-        local = 4 * part + l
+        at = h * 8 + l
+        local = l
         u = 0.1 * rows_of(wide, local, 16, 24)
         v = 0.1 * rows_of(wide, 8 + local, 16, 24)
         east_w, west_w = (0.05 - u) * mask, (0.05 + u) * mask
@@ -484,7 +506,7 @@
             kept_b[pl.ds(16 * t, 16), :] = q.astype(jnp.bfloat16)
 
     def settle(l, kept, kept_b):
-        temper = rows_of(wide, 16 + 4 * part + l, 16, 24)
+        temper = rows_of(wide, 16 + l, 16, 24)
         for c in range(0, 16, CHUNK):
             y = jnp.dot(mix[pl.ds(32 * c, 32 * CHUNK), :], kept_b[...], preferred_element_type=jnp.float32)
             for t in range(CHUNK):
@@ -493,7 +515,7 @@
                 kept[c + t] = q
                 out_ref[c + t, l] = q.astype(jnp.bfloat16)
         for a in range(4):
-            chosen[h, a, 4 * part + l] = kept[ids_ref[a]].astype(jnp.bfloat16)
+            chosen[h, a, l] = kept[ids_ref[a]].astype(jnp.bfloat16)
 
     def several(i, carry):
         pend = None
@@ -505,25 +527,27 @@
                 settle(*pend)
             pend = now
         settle(*pend)
+
+        @pl.when(step + i == 0)
+        def _():
+            pl.semaphore_wait(barrier, DST - 1)
+
+        @pl.when(step < DST - 1)
+        def _():
+            send(step, i).start()
+
         return carry
 
     lax.fori_loop(0, levels // UNROLL, several, 0)
 
-    @pl.when(step == 0)
-    def _():
-        pl.semaphore_wait(barrier, DST - 1)
-
-    @pl.when(step < 14)
-    def _():
-        send(step).start()
-
-    @pl.when(step == 15)
+    @pl.when(step == DST - 1)
     def _():
         mine = pltpu.make_async_copy(chosen.at[tile], place, own)
         mine.start()
         mine.wait()
-        for d in range(14):
-            send(d).wait()
+        for d in range(DST - 1):
+            for half in range(2):
+                send(d, half).wait()
 
 
 def chemistry(tracers, winds, north, south, east, west, base, temp, ids, points):
@@ -531,31 +555,27 @@
     hbm = pl.BlockSpec(memory_space=pl.ANY)
 
     def rows(s, i, p):
-        tile, part = tile_of_step(lax.axis_index("lon"), s)
-        return (2 * tile + part, 0, 0)
+        return (tile_of_step(lax.axis_index("lon"), s), 0, 0)
 
     def cube(s, i, p):
         return (0,) + rows(s, i, p)
-
-    def source(s, i, p):
-        return (tile_of_step(lax.axis_index("lon"), s)[0], 0, 0)
 
     return pl.pallas_call(
         chem_kernel,
         grid_spec=pltpu.PrefetchScalarGridSpec(
             num_scalar_prefetch=2,
-            grid=(16,),
+            grid=(8,),
             in_specs=[
-                pl.BlockSpec((16, 4, 16, 256), cube),
-                pl.BlockSpec((1, 384, 256), source),
-                pl.BlockSpec((4, 16, 256), rows),
-                pl.BlockSpec((4, 16, 256), rows),
+                pl.BlockSpec((16, 8, 16, 256), cube),
+                pl.BlockSpec((1, 384, 256), rows),
+                pl.BlockSpec((8, 16, 256), rows),
+                pl.BlockSpec((8, 16, 256), rows),
                 pl.BlockSpec((256, 128), whole),
                 pl.BlockSpec((256, 128), whole),
                 pl.BlockSpec((16, 16), whole),
                 pl.BlockSpec((16, 16), whole),
             ],
-            out_specs=[pl.BlockSpec((16, 4, 16, 256), cube), hbm],
+            out_specs=[pl.BlockSpec((16, 8, 16, 256), cube), hbm],
             scratch_shapes=[
                 pltpu.VMEM((2, 384, 128), jnp.float32),
                 pltpu.VMEM((256, 128), jnp.float32),
@@ -568,8 +588,8 @@
                 pltpu.VMEM((256, 256), jnp.bfloat16),
                 pltpu.VMEM((256, 256), jnp.bfloat16),
                 pltpu.VMEM((8, 4, 8, 16, 256), jnp.bfloat16),
-                pltpu.SemaphoreType.DMA((14,)),
-                pltpu.SemaphoreType.DMA((14,)),
+                pltpu.SemaphoreType.DMA((7, 2)),
+                pltpu.SemaphoreType.DMA((7, 2)),
                 pltpu.SemaphoreType.DMA,
             ],
         ),

time: 103 us -> 105 us (1.019)
  the two profiles are of different devices: /device:TPU:25 before, /device:TPU:1 now
where the time goes in v6:
time: 105 us
  Pallas kernels  92.5 us (88%)
  local copies, waits for them, and re-layouts  7.52 us (7%)
  other arithmetic  4.13 us (4%)
    pallas_call x1, Pallas kernels, winds_of(): pl.pallas_call(spectral_kernel, in_specs=[hbm, hbm, hbm, vmem, pl.BlockSp...  57.8 us
    pallas_call x1, Pallas kernels, chemistry(): pl.pallas_call(chem_kernel, grid_spec=pltpu.PrefetchScalarGridSpec(num_sc...  34.6 us
    unnamed x1, local copies, waits for them, and re-layouts  7.52 us
    convert_element_type x1, other arithmetic, body(): return (fresh, active.astype(jnp.float32))  4.13 us

profile of v6, /device:TPU:1, one launch (start us, length us, event | category | flops | bytes accessed | tf_op | source)
XLA Modules:
  0.0 104.8 jit_solution(9170039954673671414)
XLA Ops:
  0.6 57.8 %winds.1 = (bf16[8,384,256]{2,1,0:T(8,128)(2,1)}, bf16[64,16,256]{2,1,0:T(8,128)(2,1)}, bf16[64,16,256]{2,1,0:T(8,128)(2,1)}, bf16[256,128]{1,0:T(8,128)(2,1)}, bf16[256,128]{1,0:T(8,128)(2,1)}) custom-call(bf16[48,40,1280]{2,1,0:T(8,128)(2,1)} %bitcast.2, bf16[40,1280,256]{2,1,0:T(8,128)(2,1)} %leg_ref.1, bf16[16,64,16,256]{3,2,1,0:T(8,128)(2,1)} %tr_ref.3, ...), custom_call_target="tpu_custom_call" | custom-call | tf_op jit(solution)/shard_map/winds/pallas_call | solution.py:366
  58.5 34.6 %chemistry.1 = (bf16[16,64,16,256]{3,2,1,0:T(8,128)(2,1)}, bf16[4,8,16,2048]{3,2,1,0:T(8,128)(2,1)}) custom-call(s32[4]{0:T(128)} %ids_ref.1, s32[16]{0:T(128)} %pts_ref.3, bf16[16,64,16,256]{3,2,1,0:T(8,128)(2,1)} %tr_ref.3, bf16[8,384,256]{2,1,0:T(8,128)(2,1)} %get-tuple-element.9.wind_ref, bf16[64,16,256]{2,1,0:T(8,128)(2,1)} %get-tuple-element.10.north_ref, ...), custom_call_target="tpu_custom_call" | custom-call | tf_op jit(solution)/shard_map/chemistry/pallas_call | solution.py:563
  93.1 4.1 %convert_element_type.3 = f32[4,8,16,2048]{3,2,1,0:T(8,128)} convert(bf16[4,8,16,2048]{3,2,1,0:T(8,128)(2,1)} %get-tuple-element.15) | non-fusion elementwise | flops 1048576 | bytes 6291456 | tf_op jit(solution)/shard_map/convert_element_type | solution.py:612
  97.2 7.5 %copy.11 = bf16[16,64,16,256]{3,2,1,0:T(8,128)(2,1)} copy(bf16[16,64,16,256]{3,2,1,0:T(8,128)(2,1)} %get-tuple-element.18) | data formatting | bytes 16777216

commit v7 on v5

--- a/solution.py
+++ b/solution.py
@@ -17,11 +17,8 @@
 DST = 8
 MESH = pl.DeviceIdType.MESH
 TILES = ((2, 1), (2, 0), (1, 1), (3, 0), (3, 1), (1, 0), (0, 1))
-ORDER = ((2, 0), (0, 1), (2, 1), (1, 0), (3, 1), (1, 1), (3, 0))
-BANDS = (
-    (1, 2, 0), (1, 2, 1), (0, 1, 0), (1, 0, 0), (0, 3, 1), (1, 1, 0), (0, 2, 0), (1, 3, 1),
-    (0, 1, 1), (1, 0, 1), (0, 3, 0), (1, 1, 1), (0, 2, 1), (1, 3, 0), (0, 0, 1),
-)
+ORDER = ((2, 1), (0, 1), (2, 0), (1, 1), (3, 1), (1, 0), (3, 0))
+BANDS = tuple((dz, dy, dc) for dz in (1, 0) for dy in (2, 1, 3, 0) for dc in (0, 1) if dz + dy + dc)
 COS = (0.9999992006931535, -19.7389777615569, 64.92855937725766, -85.27036091136767,
        58.78399626476764, -21.059548245283555)
 SIN = (6.283184911477688, -41.3415879428884, 81.59989458670537, -76.61384581975258,
@@ -155,6 +152,11 @@
         def _():
             leg_copy(i - 3).start()
 
+        for n in range(3):
+            @pl.when(i == 2 * n + 3)
+            def _():
+                send_rows(n)
+
         side = lax.rem(i, 2)
         band_copy(i).wait()
 
@@ -181,33 +183,45 @@
 
         return carry
 
-    lax.fori_loop(0, 8, edges, 0)
-    edge[...] = cols[...].astype(jnp.bfloat16)
-    pl.semaphore_wait(barrier, SRC + DST - 2)
-
     def halo(k, src, dst, lat, lon):
         return pltpu.make_async_remote_copy(
             src_ref=src, dst_ref=dst, send_sem=sent_h.at[k], recv_sem=came_h.at[k],
             device_id=(lat, lon), device_id_type=MESH,
         )
 
-    to_north = halo(0, high, south_ref, lax.rem(g + 1, SRC), h)
-    to_south = halo(1, low, north_ref, lax.rem(g + SRC - 1, SRC), h)
-    to_east = halo(2, edge, west_ref, g, lax.rem(h + 1, DST))
-    to_west = halo(3, edge, east_ref, g, lax.rem(h + DST - 1, DST))
+    to_east = halo(0, edge, west_ref, g, lax.rem(h + 1, DST))
+    to_west = halo(1, edge, east_ref, g, lax.rem(h + DST - 1, DST))
+
+    def to_north(n):
+        rows = pl.ds(16 * n, 16)
+        return halo(2 + n, high.at[rows], south_ref.at[rows], lax.rem(g + 1, SRC), h)
+
+    def to_south(n):
+        rows = pl.ds(16 * n, 16)
+        return halo(6 + n, low.at[rows], north_ref.at[rows], lax.rem(g + SRC - 1, SRC), h)
+
+    def send_rows(n):
+        @pl.when(g < SRC - 1)
+        def _():
+            to_north(n).start()
+
+        @pl.when(g > 0)
+        def _():
+            to_south(n).start()
+
     none_south = pltpu.make_async_copy(empty, south_ref, own.at[5])
     none_north = pltpu.make_async_copy(empty, north_ref, own.at[6])
     none_west = pltpu.make_async_copy(blank_cols, west_ref, own.at[7])
     none_east = pltpu.make_async_copy(blank_cols, east_ref, own.at[8])
-    sides = (
-        (g < SRC - 1, to_north, g > 0, none_south),
-        (g > 0, to_south, g < SRC - 1, none_north),
-        (h < DST - 1, to_east, h > 0, none_west),
-        (h > 0, to_west, h < DST - 1, none_east),
-    )
-    for sends, copy, gets, fill in sides:
-        pl.when(sends)(copy.start)
-        pl.when(jnp.logical_not(gets))(fill.start)
+    fills = ((g == 0, none_south), (g == SRC - 1, none_north), (h == 0, none_west), (h == DST - 1, none_east))
+    pl.semaphore_wait(barrier, SRC + DST - 2)
+    lax.fori_loop(0, 8, edges, 0)
+    edge[...] = cols[...].astype(jnp.bfloat16)
+    send_rows(3)
+    pl.when(h < DST - 1)(to_east.start)
+    pl.when(h > 0)(to_west.start)
+    for here, fill in fills:
+        pl.when(here)(fill.start)
 
     def turn(half):
         def pair(i, carry):
@@ -333,10 +347,17 @@
         return carry
 
     lax.fori_loop(0, 4, finish, 0)
-    for sends, copy, gets, fill in sides:
-        pl.when(sends)(copy.wait_send)
-        pl.when(gets)(copy.wait_recv)
-        pl.when(jnp.logical_not(gets))(fill.wait)
+    pl.when(h < DST - 1)(to_east.wait_send)
+    pl.when(h > 0)(to_west.wait_send)
+    pl.when(h > 0)(to_east.wait_recv)
+    pl.when(h < DST - 1)(to_west.wait_recv)
+    for n in range(4):
+        pl.when(g < SRC - 1)(to_north(n).wait_send)
+        pl.when(g > 0)(to_south(n).wait_send)
+        pl.when(g > 0)(to_north(n).wait_recv)
+        pl.when(g < SRC - 1)(to_south(n).wait_recv)
+    for here, fill in fills:
+        pl.when(here)(fill.wait)
 
 
 def winds_of(spectral, legendre, tracers, wave_ids, points):
@@ -384,8 +405,8 @@
             pltpu.SemaphoreType.DMA((4, 8)),
             pltpu.SemaphoreType.DMA((4, 8)),
             pltpu.SemaphoreType.DMA((9,)),
-            pltpu.SemaphoreType.DMA((4,)),
-            pltpu.SemaphoreType.DMA((4,)),
+            pltpu.SemaphoreType.DMA((10,)),
+            pltpu.SemaphoreType.DMA((10,)),
             pltpu.SemaphoreType.DMA,
             pltpu.SemaphoreType.DMA((5,)),
             pltpu.SemaphoreType.DMA((2,)),

time: 103 us -> 101 us (0.981)
  Pallas kernels: 90.4 us -> 87.4 us
    pallas_call x1, Pallas kernels: 58.5 us -> 55.5 us  [winds_of(): pl.pallas_call(spectral_kernel, in_specs=[hbm, hbm, hbm, vmem, pl.BlockSp...]
where the time goes in v7:
time: 101 us; the launch traced here: 99.7 us
  Pallas kernels  87.4 us (87%)
  local copies, waits for them, and re-layouts  7.52 us (7%)
  other arithmetic  4.13 us (4%)
    pallas_call x1, Pallas kernels, winds_of(): pl.pallas_call(spectral_kernel, in_specs=[hbm, hbm, hbm, vmem, pl.BlockSp...  55.5 us
    pallas_call x1, Pallas kernels, chemistry(): pl.pallas_call(chem_kernel, grid_spec=pltpu.PrefetchScalarGridSpec(num_sc...  31.9 us
    unnamed x1, local copies, waits for them, and re-layouts  7.52 us
    convert_element_type x1, other arithmetic, body(): return (fresh, active.astype(jnp.float32))  4.13 us

profile of v7, /device:TPU:25, one launch (start us, length us, event | category | flops | bytes accessed | tf_op | source)
XLA Modules:
  0.0 99.7 jit_solution(10341176491547089985)
XLA Ops:
  0.6 55.5 %winds.1 = (bf16[8,384,256]{2,1,0:T(8,128)(2,1)}, bf16[64,16,256]{2,1,0:T(8,128)(2,1)}, bf16[64,16,256]{2,1,0:T(8,128)(2,1)}, bf16[256,128]{1,0:T(8,128)(2,1)}, bf16[256,128]{1,0:T(8,128)(2,1)}) custom-call(bf16[48,40,1280]{2,1,0:T(8,128)(2,1)} %bitcast.2, bf16[40,1280,256]{2,1,0:T(8,128)(2,1)} %leg_ref.1, bf16[16,64,16,256]{3,2,1,0:T(8,128)(2,1)} %tr_ref.3, ...), custom_call_target="tpu_custom_call" | custom-call | tf_op jit(solution)/shard_map/winds/pallas_call | solution.py:366
  56.1 31.9 %chemistry.1 = (bf16[16,64,16,256]{3,2,1,0:T(8,128)(2,1)}, bf16[4,8,16,2048]{3,2,1,0:T(8,128)(2,1)}) custom-call(s32[4]{0:T(128)} %ids_ref.1, s32[16]{0:T(128)} %pts_ref.3, bf16[16,64,16,256]{3,2,1,0:T(8,128)(2,1)} %tr_ref.3, bf16[8,384,256]{2,1,0:T(8,128)(2,1)} %get-tuple-element.9.wind_ref, bf16[64,16,256]{2,1,0:T(8,128)(2,1)} %get-tuple-element.10.north_ref, ...), custom_call_target="tpu_custom_call" | custom-call | tf_op jit(solution)/shard_map/chemistry/pallas_call | solution.py:564
  88.1 4.1 %convert_element_type.3 = f32[4,8,16,2048]{3,2,1,0:T(8,128)} convert(bf16[4,8,16,2048]{3,2,1,0:T(8,128)(2,1)} %get-tuple-element.15) | non-fusion elementwise | flops 1048576 | bytes 6291456 | tf_op jit(solution)/shard_map/convert_element_type | solution.py:613
  92.2 7.5 %copy.11 = bf16[16,64,16,256]{3,2,1,0:T(8,128)(2,1)} copy(bf16[16,64,16,256]{3,2,1,0:T(8,128)(2,1)} %get-tuple-element.18) | data formatting | bytes 16777216

commit v8 on v7

--- a/solution.py
+++ b/solution.py
@@ -17,7 +17,7 @@
 DST = 8
 MESH = pl.DeviceIdType.MESH
 TILES = ((2, 1), (2, 0), (1, 1), (3, 0), (3, 1), (1, 0), (0, 1))
-ORDER = ((2, 1), (0, 1), (2, 0), (1, 1), (3, 1), (1, 0), (3, 0))
+ORDER = ((2, 0), (0, 1), (2, 1), (1, 0), (3, 1), (1, 1), (3, 0))
 BANDS = tuple((dz, dy, dc) for dz in (1, 0) for dy in (2, 1, 3, 0) for dc in (0, 1) if dz + dy + dc)
 COS = (0.9999992006931535, -19.7389777615569, 64.92855937725766, -85.27036091136767,
        58.78399626476764, -21.059548245283555)

time: 101 us -> 102 us (level)
  no operation moved by 1% of the time
where the time goes in v8:
time: 102 us; the launch traced here: 99.8 us
  Pallas kernels  87.5 us (86%)
  local copies, waits for them, and re-layouts  7.52 us (7%)
  other arithmetic  4.13 us (4%)
    pallas_call x1, Pallas kernels, winds_of(): pl.pallas_call(spectral_kernel, in_specs=[hbm, hbm, hbm, vmem, pl.BlockSp...  55.5 us
    pallas_call x1, Pallas kernels, chemistry(): pl.pallas_call(chem_kernel, grid_spec=pltpu.PrefetchScalarGridSpec(num_sc...  32 us
    unnamed x1, local copies, waits for them, and re-layouts  7.52 us
    convert_element_type x1, other arithmetic, body(): return (fresh, active.astype(jnp.float32))  4.13 us

profile of v8, /device:TPU:25, one launch (start us, length us, event | category | flops | bytes accessed | tf_op | source)
XLA Modules:
  0.0 99.8 jit_solution(170860175286333438)
XLA Ops:
  0.6 55.5 %winds.1 = (bf16[8,384,256]{2,1,0:T(8,128)(2,1)}, bf16[64,16,256]{2,1,0:T(8,128)(2,1)}, bf16[64,16,256]{2,1,0:T(8,128)(2,1)}, bf16[256,128]{1,0:T(8,128)(2,1)}, bf16[256,128]{1,0:T(8,128)(2,1)}) custom-call(bf16[48,40,1280]{2,1,0:T(8,128)(2,1)} %bitcast.2, bf16[40,1280,256]{2,1,0:T(8,128)(2,1)} %leg_ref.1, bf16[16,64,16,256]{3,2,1,0:T(8,128)(2,1)} %tr_ref.3, ...), custom_call_target="tpu_custom_call" | custom-call | tf_op jit(solution)/shard_map/winds/pallas_call | solution.py:366
  56.1 32.0 %chemistry.1 = (bf16[16,64,16,256]{3,2,1,0:T(8,128)(2,1)}, bf16[4,8,16,2048]{3,2,1,0:T(8,128)(2,1)}) custom-call(s32[4]{0:T(128)} %ids_ref.1, s32[16]{0:T(128)} %pts_ref.3, bf16[16,64,16,256]{3,2,1,0:T(8,128)(2,1)} %tr_ref.3, bf16[8,384,256]{2,1,0:T(8,128)(2,1)} %get-tuple-element.9.wind_ref, bf16[64,16,256]{2,1,0:T(8,128)(2,1)} %get-tuple-element.10.north_ref, ...), custom_call_target="tpu_custom_call" | custom-call | tf_op jit(solution)/shard_map/chemistry/pallas_call | solution.py:564
  88.1 4.1 %convert_element_type.3 = f32[4,8,16,2048]{3,2,1,0:T(8,128)} convert(bf16[4,8,16,2048]{3,2,1,0:T(8,128)(2,1)} %get-tuple-element.15) | non-fusion elementwise | flops 1048576 | bytes 6291456 | tf_op jit(solution)/shard_map/convert_element_type | solution.py:613
  92.2 7.5 %copy.11 = bf16[16,64,16,256]{3,2,1,0:T(8,128)(2,1)} copy(bf16[16,64,16,256]{3,2,1,0:T(8,128)(2,1)} %get-tuple-element.18) | data formatting | bytes 16777216
